TPU v7x, 512 devices: a whole 4x4x16 slice. The times are simulated.
512 devices in a mesh: slab: 128 (over y, z, core), tile: 4 (over x).
Axes of the slice: x: 4, y: 4, z: 16, core: 2. Of those that a mesh axis runs over, the one named last changes fastest.
Arguments:
- tokens: bfloat16 [1024, 1024, 128], P('slab', 'tile'), may hold values from -6 to 6
- conv_weight: float32 [3, 3, 128], replicated, may hold values from -2.5 to 2.5
- occupancy: int32 [16, 16], replicated, may hold values 0 or 1
- row_gain: float32 [128], replicated, may hold values from 0.1 to 1.9
- row_qkv: bfloat16 [128, 384], replicated, may hold values from -5 to 5
- row_out: bfloat16 [128, 128], replicated, may hold values from -0.5 to 0.5
- col_gain: float32 [128], replicated, may hold values from 0.1 to 1.9
- col_qkv: bfloat16 [128, 384], replicated, may hold values from -5 to 5
- col_out: bfloat16 [128, 128], replicated, may hold values from -0.5 to 0.5
Outputs:
- mixed: bfloat16 [1024, 1024, 128], P(None, ('tile', 'slab'))
All inputs are finite; a program needn't handle non-finite values.
Results may differ from a plain program's by a relative error of at most 0.02.
Values may be sent and summed in bfloat16 or wider, within the bound.
A program may use at most 64 MiB of HBM per device.

v0:
```python
import math

import jax
import jax.numpy as jnp
from jax import lax
from jax.sharding import PartitionSpec as P

HEAD_DIM = 32
COL_REACH = 128


def padded_2(block, sides, width):
    for axis, dim in sides:
        count = lax.axis_size(axis)
        forward = [(i, i + 1) for i in range(count - 1)]
        backward = [(target, source) for source, target in forward]
        low = lax.ppermute(
            lax.slice_in_dim(block, block.shape[dim] - width, None, axis=dim), axis, forward
        )
        high = lax.ppermute(lax.slice_in_dim(block, 0, width, axis=dim), axis, backward)
        block = jnp.concatenate([low, block, high], axis=dim)
    return block


def attend(queries, key_block, value_block, query_pos, key_pos, query_ok, key_ok, band_reach):
    query_count = queries.shape[0]
    key_count = key_block.shape[0]
    head_count = queries.shape[1] // HEAD_DIM
    query_heads = queries.reshape(query_count, head_count, HEAD_DIM)
    key_heads = key_block.reshape(key_count, head_count, HEAD_DIM)
    value_heads = value_block.reshape(key_count, head_count, HEAD_DIM)
    scores = jnp.einsum(
        "qhd,khd->hqk", query_heads, key_heads, preferred_element_type=jnp.float32
    ) / math.sqrt(HEAD_DIM)
    offsets = query_pos[:, None] - key_pos[None, :]
    allowed = (jnp.abs(offsets) < band_reach) & ((key_ok[None, :] > 0) | (offsets == 0))
    scores = jnp.where(allowed[None], scores, jnp.float32(-1e30))
    row_max = jnp.max(scores, axis=-1, keepdims=True)
    exp_terms = jnp.exp(scores - row_max)
    row_total = jnp.sum(exp_terms, axis=-1, keepdims=True)
    weights = (exp_terms / row_total).astype(jnp.bfloat16)
    mixture = jnp.einsum("hqk,khd->qhd", weights, value_heads, preferred_element_type=jnp.float32)
    mixture = mixture * query_ok[:, None, None].astype(jnp.float32)
    return mixture.reshape(query_count, head_count * HEAD_DIM).astype(jnp.bfloat16)


def attend_line(projected, line_ok, band_reach):
    line_len = projected.shape[0]
    model_width = projected.shape[1] // 3
    block_rows = min(256, line_len)
    block_count = line_len // block_rows
    queries = projected[:, :model_width]
    key_value = jnp.pad(projected[:, model_width:], ((band_reach, band_reach), (0, 0)))
    padded_ok = jnp.pad(line_ok, (band_reach, band_reach))
    positions = jnp.arange(line_len + 2 * band_reach, dtype=jnp.int32) - band_reach

    def one_block(block_index):
        block_start = block_index * block_rows
        query_part = lax.dynamic_slice_in_dim(queries, block_start, block_rows, 0)
        query_ok = lax.dynamic_slice_in_dim(line_ok, block_start, block_rows, 0)
        query_pos = lax.dynamic_slice_in_dim(positions, block_start + band_reach, block_rows, 0)
        kv_part = lax.dynamic_slice_in_dim(key_value, block_start, block_rows + 2 * band_reach, 0)
        key_ok = lax.dynamic_slice_in_dim(padded_ok, block_start, block_rows + 2 * band_reach, 0)
        key_pos = lax.dynamic_slice_in_dim(positions, block_start, block_rows + 2 * band_reach, 0)
        return attend(
            query_part,
            kv_part[:, :model_width],
            kv_part[:, model_width:],
            query_pos,
            key_pos,
            query_ok,
            key_ok,
            band_reach,
        )

    blocks = lax.map(one_block, jnp.arange(block_count, dtype=jnp.int32))
    return blocks.reshape(line_len, model_width)


def layer_norm(stream, gain):
    values32 = stream.astype(jnp.float32)
    center = jnp.mean(values32, axis=-1, keepdims=True)
    centered = values32 - center
    spread = jnp.mean(centered * centered, axis=-1, keepdims=True)
    return (centered * lax.rsqrt(spread + 1e-05) * gain).astype(jnp.bfloat16)


def column_part(stream, col_ok, gain, qkv_weight, out_weight):
    normed = layer_norm(stream, gain)
    projected = jnp.dot(normed, qkv_weight, preferred_element_type=jnp.float32).astype(jnp.bfloat16)
    by_column = jnp.moveaxis(projected, 1, 0)
    ok_column = jnp.moveaxis(col_ok, 1, 0)
    mixture = lax.map(
        lambda pieces: attend_line(pieces[0], pieces[1], COL_REACH), (by_column, ok_column)
    )
    mixture = jnp.moveaxis(mixture, 0, 1)
    update = jnp.dot(mixture, out_weight, preferred_element_type=jnp.float32)
    return (stream.astype(jnp.float32) + update).astype(jnp.bfloat16)


def local(tokens, conv_weight, occupancy, row_gain, row_qkv, row_out, col_gain, col_qkv, col_out):
    row_count, length, model_width = tokens.shape
    slab_count = lax.axis_size("slab")
    slab_at = lax.axis_index("slab")
    tile_at = lax.axis_index("tile")
    height = row_count * slab_count
    block_size = height // occupancy.shape[0]
    band_reach = min(128, length)
    col_count = length // slab_count
    padded = padded_2(tokens, (("slab", 0), ("tile", 1)), 1)
    padded32 = padded.astype(jnp.float32)
    convolved = padded32[1 : 1 + row_count, 1 : 1 + length]
    for shift_row in range(3):
        for shift_col in range(3):
            convolved = (
                convolved
                + conv_weight[shift_row, shift_col]
                * padded32[shift_row : shift_row + row_count, shift_col : shift_col + length]
            )
    stream = convolved.astype(jnp.bfloat16)
    normed = layer_norm(stream, row_gain)
    projected = jnp.dot(normed, row_qkv, preferred_element_type=jnp.float32).astype(jnp.bfloat16)
    queries = projected[..., :model_width]
    line_ids = (slab_at * row_count + jnp.arange(row_count, dtype=jnp.int32)) // block_size
    selector = (
        line_ids[:, None] == jnp.arange(occupancy.shape[0], dtype=jnp.int32)[None, :]
    ).astype(jnp.int32)
    occ_rows = jnp.dot(selector, occupancy)
    occ_line = jnp.repeat(occ_rows, block_size, axis=1)
    occ_wide = jnp.pad(occ_line, ((0, 0), (band_reach, band_reach)))
    key_ok = lax.dynamic_slice_in_dim(occ_wide, tile_at * length, length + 2 * band_reach, 1)
    query_ok = key_ok[:, band_reach : band_reach + length]
    kv_wide = padded_2(projected[..., model_width:], (("tile", 1),), band_reach)
    query_pos = tile_at * length + jnp.arange(length, dtype=jnp.int32)
    key_pos = tile_at * length - band_reach + jnp.arange(length + 2 * band_reach, dtype=jnp.int32)

    def row_attend(pieces):
        query_row, kv_row, qok_row, kok_row = pieces
        return attend(
            query_row,
            kv_row[:, :model_width],
            kv_row[:, model_width:],
            query_pos,
            key_pos,
            qok_row,
            kok_row,
            band_reach,
        )

    mixture = lax.map(row_attend, (queries, kv_wide, query_ok, key_ok))
    after_rows = (
        stream.astype(jnp.float32) + jnp.dot(mixture, row_out, preferred_element_type=jnp.float32)
    ).astype(jnp.bfloat16)
    columns = lax.all_to_all(after_rows, "slab", split_axis=1, concat_axis=0, tiled=True)
    col_ids = (
        tile_at * length + slab_at * col_count + jnp.arange(col_count, dtype=jnp.int32)
    ) // block_size
    col_selector = (
        jnp.arange(occupancy.shape[1], dtype=jnp.int32)[:, None] == col_ids[None, :]
    ).astype(jnp.int32)
    occ_blocks = jnp.dot(occupancy, col_selector)
    col_ok = jnp.repeat(occ_blocks, block_size, axis=0)
    result = column_part(columns, col_ok, col_gain, col_qkv, col_out)
    return result


def solution(mesh):
    return jax.shard_map(
        local,
        mesh=mesh,
        in_specs=(P("slab", "tile", None), P(), P(), P(), P(), P(), P(), P(), P()),
        out_specs=P(None, ("tile", "slab"), None),
        check_vma=False,
    )
```

profile of v0, /device:TPU:1, one launch (start us, length us, event | category | flops | bytes accessed | tf_op | source)
XLA Modules:
  0.0 189.0 jit_solution(11534198888149711325)
XLA Ops:
  0.9 4.9 %collective-permute-start = (bf16[1,256,128]{2,1,0:T(8,128)(2,1)S(1)}, bf16[1,256,128]{2,1,0:T(8,128)(2,1)S(1)}, u32[]{:S(2)}, u32[]{:S(2)}) collective-permute-start(bf16[1,256,128]{2,1,0:T(8,128)(2,1)S(1)} %get-tuple-element.356), channel_id=1, source_target_pairs={{0,4},{4,8},{8,12},{12,16},{16,20},{20,24},{24,28},{28,32},{32,36}... | collective-permute-start | bytes 196616 | tf_op jit(solution)/shard_map/ppermute | solution.py:17
  5.9 5.1 %collective-permute-start.1 = (bf16[1,256,128]{2,1,0:T(8,128)(2,1)S(1)}, bf16[1,256,128]{2,1,0:T(8,128)(2,1)S(1)}, u32[]{:S(2)}, u32[]{:S(2)}) collective-permute-start(bf16[1,256,128]{2,1,0:T(8,128)(2,1)S(1)} %get-tuple-element.355), channel_id=1, source_target_pairs={{4,0},{8,4},{12,8},{16,12},{20,16},{24,20},{28,24},{32,28},{36,32}... | collective-permute-start | bytes 196616 | tf_op jit(solution)/shard_map/ppermute | solution.py:20
  11.0 1.1 constant_dynamic-update-slice_fusion.3
  12.2 2.4 %collective-permute-start.2 = (bf16[10,1,128]{2,1,0:T(2,128)(2,1)S(1)}, bf16[10,1,128]{2,1,0:T(2,128)(2,1)S(1)}, u32[]{:S(2)}, u32[]{:S(2)}) collective-permute-start(bf16[10,1,128]{2,1,0:T(2,128)(2,1)S(1)} %get-tuple-element.353), channel_id=1, source_target_pairs={{0,1},{1,2},{2,3},{4,5},{5,6},{6,7},{8,9},{9,10},{10,11},{12,13},{... | collective-permute-start | bytes 7688 | tf_op jit(solution)/shard_map/ppermute | solution.py:17
  14.6 1.3 collective-permute-start.3
  16.8 2.2 %collective-permute-done.3 = bf16[10,1,128]{2,1,0:T(2,128)(2,1)S(1)} collective-permute-done((bf16[10,1,128]{2,1,0:T(2,128)(2,1)S(1)}, bf16[10,1,128]{2,1,0:T(2,128)(2,1)S(1)}, u32[]{:S(2)}, u32[]{:S(2)}) %collective-permute-start.3) | collective-permute-done | bytes 2592 | tf_op jit(solution)/shard_map/ppermute | solution.py:20
  19.1 1.2 convert_reduce_fusion
  21.0 1.0 convolution_convert_fusion.1
  22.1 1.0 fusion.83
  23.0 3.9 %collective-permute-start.4 = (bf16[8,128,256]{2,1,0:T(8,128)(2,1)}, bf16[8,128,256]{2,1,0:T(8,128)(2,1)}, u32[]{:S(2)}, u32[]{:S(2)}) collective-permute-start(bf16[8,128,256]{2,1,0:T(8,128)(2,1)} %get-tuple-element.351), channel_id=1, source_target_pairs={{0,1},{1,2},{2,3},{4,5},{5,6},{6,7},{8,9},{9,10},{10,11},{12,13},{... | collective-permute-start | bytes 1572872 | tf_op jit(solution)/shard_map/ppermute | solution.py:17
  26.9 1.3 collective-permute-start.5
  28.8 8.9 %collective-permute-done.4 = bf16[8,128,256]{2,1,0:T(8,128)(2,1)} collective-permute-done((bf16[8,128,256]{2,1,0:T(8,128)(2,1)}, bf16[8,128,256]{2,1,0:T(8,128)(2,1)}, u32[]{:S(2)}, u32[]{:S(2)}) %collective-permute-start.4) | collective-permute-done | bytes 524320 | tf_op jit(solution)/shard_map/ppermute | solution.py:17
  37.7 4.7 %collective-permute-done.5 = bf16[8,128,256]{2,1,0:T(8,128)(2,1)} collective-permute-done((bf16[8,128,256]{2,1,0:T(8,128)(2,1)S(1)}, bf16[8,128,256]{2,1,0:T(8,128)(2,1)}, u32[]{:S(2)}, u32[]{:S(2)}) %collective-permute-start.5) | collective-permute-done | bytes 524320 | tf_op jit(solution)/shard_map/ppermute | solution.py:20
  42.4 2.7 %pad_maximum_fusion = bf16[8,512,256]{2,1,0:T(8,128)(2,1)} fusion(bf16[8,128,256]{2,1,0:T(8,128)(2,1)} %collective-permute-done.5, bf16[8,256,256]{2,1,0:T(8,128)(2,1)S(1)} %slice.161, bf16[8,128,256]{2,1,0:T(8,128)(2,1)} %collective-permute-done.4), kind=kLoop, calls=%fused_computation.61 | loop fusion | flops 6291456 | bytes 4194304 | tf_op jit(solution)/shard_map/concatenate | solution.py:21
  45.1 29.7 %while.45 = (s32[]{:T(128)}, bf16[8,256,128]{1,2,0:T(8,128)(2,1)S(1)}, bf16[8,512,256]{2,1,0:T(8,128)(2,1)}, s32[8,512]{1,0:T(8,128)S(1)}, bf16[8,256,128]{2,1,0...) while((s32[]{:T(128)}, bf16[8,256,128]{1,2,0:T(8,128)(2,1)S(1)}, ...), condition=%wide.region_5.6_spmd.clone, body=%wide.region_2.5_spmd.clone.sunk | while | flops 106237440 | bytes 2969721 | solution.py:150
  46.7 1.0 fusion.124
  47.7 1.1 fusion.126
  51.4 1.1 fusion.126
  55.1 1.1 fusion.126
  58.8 1.1 fusion.126
  62.5 1.1 fusion.126
  66.2 1.1 fusion.126
  69.9 1.1 fusion.126
  73.7 1.1 fusion.126
  75.1 1.1 copy.40
  76.3 19.1 %all-to-all-start = ((bf16[8,256,128]{2,0,1:T(8,128)(2,1)}), bf16[8,256,128]{2,0,1:T(8,128)(2,1)S(1)}, u32[]{:S(2)}, u32[]{:S(2)}) async-start(bf16[8,256,128]{2,0,1:T(8,128)(2,1)} %copy.40), calls=%async_computation | async-start | bytes 1048576 | tf_op jit(solution)/shard_map/all_to_all | solution.py:154
  95.7 32.8 %all-to-all-done = bf16[8,256,128]{2,0,1:T(8,128)(2,1)S(1)} async-done(((bf16[8,256,128]{2,0,1:T(8,128)(2,1)}), bf16[8,256,128]{2,0,1:T(8,128)(2,1)S(1)}, u32[]{:S(2)}, u32[]{:S(2)}) %all-to-all-start) | async-done | bytes 524320 | tf_op jit(solution)/shard_map/all_to_all | solution.py:154
  128.6 1.1 fusion.78
  129.8 1.5 copy.65
  131.9 14.7 %multiply_reduce_fusion = f32[128,8,2]{2,0,1:T(8,128)S(1)} fusion(f32[128,8,2]{2,0,1:T(8,128)S(1)} %copy.45, f32[8,128,2,128]{3,0,2,1:T(8,128)S(1)} %bitcast_convert_fusion), kind=kLoop, calls=%fused_computation.100 | loop fusion | flops 784384 | bytes 1064960 | tf_op jit(solution)/shard_map/reduce_sum | solution.py:84
  147.2 2.2 %fusion.41 = bf16[2,1024,384]{2,1,0:T(8,128)(2,1)S(1)} fusion(f32[128,8,2,128]{3,2,0,1:T(2,128)} %bitcast.154, f32[128]{0:T(128)S(1)} %copy-done.7, f32[1024,2]{0,1:T(2,128)S(1)} %rsqrt.21, f32[1024,2]{0,1:T(2,128)S(1)} %div.73, bf16[128,384]{1,0:T(8,128)(2,1)S(1)} %copy-done.2), kind=kOutput, calls=%fused_computation.67 | convolution fusion | flops 203161600 | bytes 2736640 | tf_op jit(solution)/shard_map/dot_general | solution.py:90
  149.4 36.1 %while.44 = (s32[]{:T(128)}, bf16[2,1024,128]{2,1,0:T(8,128)(2,1)}, bf16[2,1024,384]{2,1,0:T(8,128)(2,1)S(1)}, s32[2,1024]{1,0:T(2,128)S(1)}, s32[]{:T(128)}, /*...) while((s32[]{:T(128)}, bf16[2,1024,128]{2,1,0:T(8,128)(2,1)}, ...), condition=%wide.region_13.14_spmd, body=%wide.region_8.13_spmd.sunk | while | flops 106237968 | bytes 8370293 | solution.py:93
  150.0 16.7 %while.46 = (s32[]{:T(128)}, bf16[4,256,128]{2,1,0:T(8,128)(2,1)S(1)}, s32[4]{0:T(128)S(1)}, bf16[1280,256]{0,1:T(8,128)(2,1)S(1)}, s32[1280]{0:T(1024)S(1)}, /*...) while((s32[]{:T(128)}, ...), condition=%wide.region_12.12_spmd.clone, body=%wide.region_9.11_spmd.clone.sunk | while | flops 106236688 | bytes 1924418 | solution.py:76
  152.9 1.1 fusion.134
  157.1 1.1 fusion.134
  161.3 1.1 fusion.134
  165.5 1.1 fusion.134
  168.1 16.7 %while.46 = (s32[]{:T(128)}, bf16[4,256,128]{2,1,0:T(8,128)(2,1)S(1)}, s32[4]{0:T(128)S(1)}, bf16[1280,256]{0,1:T(8,128)(2,1)S(1)}, s32[1280]{0:T(1024)S(1)}, /*...) while((s32[]{:T(128)}, ...), condition=%wide.region_12.12_spmd.clone, body=%wide.region_9.11_spmd.clone.sunk | while | flops 106236688 | bytes 1924418 | solution.py:76
  170.0 1.0 fusion.133
  171.0 1.1 fusion.134
  174.1 1.0 fusion.133
  175.2 1.1 fusion.134
  178.3 1.0 fusion.133
  179.4 1.1 fusion.134
  182.5 1.0 fusion.133
  183.6 1.1 fusion.134
  185.5 2.1 %fusion.43 = bf16[1024,2,128]{2,0,1:T(8,128)(2,1)S(1)} fusion(f32[128,8,2,128]{3,2,0,1:T(2,128)} %bitcast.155, bf16[2,1024,128]{2,1,0:T(8,128)(2,1)} %get-tuple-element.223, bf16[128,128]{1,0:T(8,128)(2,1)S(1)} %copy-done.3), kind=kOutput, calls=%fused_computation.70 | convolution fusion | flops 67633152 | bytes 2129920 | tf_op jit(solution)/shard_map/dot_general | solution.py:97
  187.7 1.3 copy.49
  (255 shorter events, 42.5 us)
Async XLA Ops:
  0.0 21.0 %copy-start = (bf16[128,384]{1,0:T(8,128)(2,1)S(1)}, bf16[128,384]{1,0:T(8,128)(2,1)}, u32[]{:S(2)}) copy-start(bf16[128,384]{1,0:T(8,128)(2,1)} %param.19) | copy-start | bytes 294916
  0.9 10.1 %collective-permute-start = (bf16[1,256,128]{2,1,0:T(8,128)(2,1)S(1)}, bf16[1,256,128]{2,1,0:T(8,128)(2,1)S(1)}, u32[]{:S(2)}, u32[]{:S(2)}) collective-permute-start(bf16[1,256,128]{2,1,0:T(8,128)(2,1)S(1)} %get-tuple-element.356), channel_id=1, source_target_pairs={{0,4},{4,8},{8,12},{12,16},{16,20},{20,24},{24,28},{28,32},{32,36}... | collective-permute-start | bytes 196616 | tf_op jit(solution)/shard_map/ppermute | solution.py:17
  5.9 6.3 %collective-permute-start.1 = (bf16[1,256,128]{2,1,0:T(8,128)(2,1)S(1)}, bf16[1,256,128]{2,1,0:T(8,128)(2,1)S(1)}, u32[]{:S(2)}, u32[]{:S(2)}) collective-permute-start(bf16[1,256,128]{2,1,0:T(8,128)(2,1)S(1)} %get-tuple-element.355), channel_id=1, source_target_pairs={{4,0},{8,4},{12,8},{16,12},{20,16},{24,20},{28,24},{32,28},{36,32}... | collective-permute-start | bytes 196616 | tf_op jit(solution)/shard_map/ppermute | solution.py:20
  12.2 4.6 %collective-permute-start.2 = (bf16[10,1,128]{2,1,0:T(2,128)(2,1)S(1)}, bf16[10,1,128]{2,1,0:T(2,128)(2,1)S(1)}, u32[]{:S(2)}, u32[]{:S(2)}) collective-permute-start(bf16[10,1,128]{2,1,0:T(2,128)(2,1)S(1)} %get-tuple-element.353), channel_id=1, source_target_pairs={{0,1},{1,2},{2,3},{4,5},{5,6},{6,7},{8,9},{9,10},{10,11},{12,13},{... | collective-permute-start | bytes 7688 | tf_op jit(solution)/shard_map/ppermute | solution.py:17
  14.6 4.4 %collective-permute-start.3 = (bf16[10,1,128]{2,1,0:T(2,128)(2,1)S(1)}, bf16[10,1,128]{2,1,0:T(2,128)(2,1)S(1)}, u32[]{:S(2)}, u32[]{:S(2)}) collective-permute-start(bf16[10,1,128]{2,1,0:T(2,128)(2,1)S(1)} %get-tuple-element.354), channel_id=1, source_target_pairs={{1,0},{2,1},{3,2},{5,4},{6,5},{7,6},{9,8},{10,9},{11,10},{13,12},{... | collective-permute-start | bytes 7688 | tf_op jit(solution)/shard_map/ppermute | solution.py:20
  19.1 1.9 copy-start.6
  21.0 7.3 %copy-start.5 = (s32[16,16]{1,0:T(8,128)S(1)}, s32[16,16]{1,0:T(8,128)}, u32[]{:S(2)}) copy-start(s32[16,16]{1,0:T(8,128)} %param.17) | copy-start | bytes 3076
  22.1 6.7 %copy-start.1 = (bf16[8,256,384]{2,1,0:T(8,128)(2,1)}, bf16[8,256,384]{2,1,0:T(8,128)(2,1)S(1)}, u32[]{:S(2)}) copy-start(bf16[8,256,384]{2,1,0:T(8,128)(2,1)S(1)} %convolution_convert_fusion.1) | copy-start | bytes 4718596
  23.0 14.6 %collective-permute-start.4 = (bf16[8,128,256]{2,1,0:T(8,128)(2,1)}, bf16[8,128,256]{2,1,0:T(8,128)(2,1)}, u32[]{:S(2)}, u32[]{:S(2)}) collective-permute-start(bf16[8,128,256]{2,1,0:T(8,128)(2,1)} %get-tuple-element.351), channel_id=1, source_target_pairs={{0,1},{1,2},{2,3},{4,5},{5,6},{6,7},{8,9},{9,10},{10,11},{12,13},{... | collective-permute-start | bytes 1572872 | tf_op jit(solution)/shard_map/ppermute | solution.py:17
  26.9 15.4 %collective-permute-start.5 = (bf16[8,128,256]{2,1,0:T(8,128)(2,1)S(1)}, bf16[8,128,256]{2,1,0:T(8,128)(2,1)}, u32[]{:S(2)}, u32[]{:S(2)}) collective-permute-start(bf16[8,128,256]{2,1,0:T(8,128)(2,1)S(1)} %get-tuple-element.352), channel_id=1, source_target_pairs={{1,0},{2,1},{3,2},{5,4},{6,5},{7,6},{9,8},{10,9},{11,10},{13,12},{... | collective-permute-start | bytes 1572872 | tf_op jit(solution)/shard_map/ppermute | solution.py:20
  28.7 16.3 %slice-start = ((bf16[8,256,384]{2,1,0:T(8,128)(2,1)}), bf16[8,256,128]{2,1,0:T(8,128)(2,1)S(1)}, s32[]{:S(2)}) async-start(bf16[8,256,384]{2,1,0:T(8,128)(2,1)} %copy-done.1), calls=%async_computation.1 | async-start | bytes 1048576 | tf_op jit(solution)/shard_map/slice | solution.py:123
  45.1 29.7 %copy-start.4 = (bf16[128,128]{1,0:T(8,128)(2,1)S(1)}, bf16[128,128]{1,0:T(8,128)(2,1)}, u32[]{:S(2)}) copy-start(bf16[128,128]{1,0:T(8,128)(2,1)} %param.20) | copy-start | bytes 98308
  76.3 52.3 %all-to-all-start = ((bf16[8,256,128]{2,0,1:T(8,128)(2,1)}), bf16[8,256,128]{2,0,1:T(8,128)(2,1)S(1)}, u32[]{:S(2)}, u32[]{:S(2)}) async-start(bf16[8,256,128]{2,0,1:T(8,128)(2,1)} %copy.40), calls=%async_computation | async-start | bytes 1048576 | tf_op jit(solution)/shard_map/all_to_all | solution.py:154
  131.3 15.9 %copy-start.2 = (bf16[128,384]{1,0:T(8,128)(2,1)S(1)}, bf16[128,384]{1,0:T(8,128)(2,1)}, u32[]{:S(2)}) copy-start(bf16[128,384]{1,0:T(8,128)(2,1)} %param.22) | copy-start | bytes 294916
  131.3 15.9 %copy-start.7 = (f32[128]{0:T(128)S(1)}, f32[128]{0:T(128)}, u32[]{:S(2)}) copy-start(f32[128]{0:T(128)} %param.21) | copy-start | bytes 1540
  149.4 36.2 %copy-start.3 = (bf16[128,128]{1,0:T(8,128)(2,1)S(1)}, bf16[128,128]{1,0:T(8,128)(2,1)}, u32[]{:S(2)}) copy-start(bf16[128,128]{1,0:T(8,128)(2,1)} %param.23) | copy-start | bytes 98308
where the time goes:
time: 190 us; the launch traced here: 189 us
  waiting for transfers between devices  48.6 us (26%)
  matrix products  38.5 us (20%)
  starting transfers between devices  38 us (20%)
  local copies, waits for them, and re-layouts  30.4 us (16%)
  other arithmetic  26.6 us (14%)
  loops' own time  6.54 us (3%)
    all_to_all x1, waiting for transfers between devices, local(): lax.all_to_all(after_rows, 'slab', split_axis=1, concat_axis=0, tiled=True)  32.8 us
    all_to_all x1, starting transfers between devices, local(): lax.all_to_all(after_rows, 'slab', split_axis=1, concat_axis=0, tiled=True)  19.1 us
    dot_general x16, matrix products, attend(): jnp.einsum('hqk,khd->qhd', weights, value_heads, preferred_element_type=j...  16.9 us
    sub x16, matrix products, attend(): exp_terms = jnp.exp(scores - row_max)  15.5 us
    reduce_sum x2, other arithmetic, layer_norm(): spread = jnp.mean(centered * centered, axis=-1, keepdims=True)  15.4 us
    ppermute x3, starting transfers between devices, padded_2(): lax.ppermute(lax.slice_in_dim(block, block.shape[dim] - width, None, axis...  11.2 us
    dynamic_slice x32, local copies, waits for them, and re-layouts, local(): mixture = lax.map(row_attend, (queries, kv_wide, query_ok, key_ok))  9.88 us
    ppermute x3, waiting for transfers between devices, padded_2(): lax.ppermute(lax.slice_in_dim(block, block.shape[dim] - width, None, axis...  8.91 us
  transfers between devices with their start and end apart: 7, of which 4 were waited for; matrix products, arithmetic and copies ran while one was open for 1% of the time, Pallas kernels for 0%

commit v1 on v0

v1 whole, which is shorter than its diff:
```python
import math

import jax
import jax.numpy as jnp
from jax import lax
from jax.experimental import pallas as pl
from jax.experimental.pallas import tpu as pltpu
from jax.sharding import PartitionSpec as P

HEAD_DIM = 32
HEADS = 4
BLOCK = 64
REACH = 128
KEYS = 3 * REACH
NEG = -1e30
SCALE = math.log2(math.e) / math.sqrt(HEAD_DIM)


def norm(values32, gain):
    center = jnp.mean(values32, axis=-1, keepdims=True)
    centered = values32 - center
    spread = jnp.mean(centered * centered, axis=-1, keepdims=True)
    return (centered * lax.rsqrt(spread + 1e-05) * gain).astype(jnp.bfloat16)


def block_bias(key_occupied):
    lane = lax.broadcasted_iota(jnp.int32, (1, KEYS), 1) // BLOCK
    key_bias = jnp.zeros((1, KEYS), jnp.float32)
    for index, occupied in enumerate(key_occupied):
        value = jnp.where(occupied > 0, jnp.float32(0.0), jnp.float32(NEG))
        key_bias = jnp.where(lane == index, value, key_bias)
    query = lax.broadcasted_iota(jnp.int32, (REACH, KEYS), 0)
    key = lax.broadcasted_iota(jnp.int32, (REACH, KEYS), 1) - REACH
    offset = query - key
    bias = jnp.where(jnp.abs(offset) < REACH, jnp.broadcast_to(key_bias, offset.shape), NEG)
    return jnp.where(offset == 0, 0.0, bias)


def heads_of(lane_shape):
    return lax.broadcasted_iota(jnp.int32, lane_shape, 1) // HEAD_DIM


def attend_block(queries, keys, values_ones, bias, query_occupied):
    head = heads_of((REACH, 128))
    zero = jnp.zeros_like(queries)
    stacked = jnp.concatenate([jnp.where(head == h, queries, zero) for h in range(HEADS)], axis=0)
    scores = lax.dot_general(
        stacked, keys, (((1,), (1,)), ((), ())), preferred_element_type=jnp.float32
    )
    parts = []
    for h in range(HEADS):
        part = scores[h * REACH : (h + 1) * REACH] + bias
        top = jnp.max(part, axis=-1, keepdims=True)
        parts.append(jnp.exp2(part - top).astype(jnp.bfloat16))
    weights = jnp.concatenate(parts, axis=0)
    both = jnp.dot(weights, values_ones, preferred_element_type=jnp.float32)
    mixture, total = both[:REACH, :128], both[:REACH, 128:]
    for h in range(1, HEADS):
        rows = both[h * REACH : (h + 1) * REACH]
        mixture = jnp.where(head == h, rows[:, :128], mixture)
        total = jnp.where(head == h, rows[:, 128:], total)
    mixture = mixture / total
    row = lax.broadcasted_iota(jnp.int32, (REACH, 128), 0)
    occupied = jnp.where(row < BLOCK, query_occupied[0], query_occupied[1])
    return (mixture * occupied.astype(jnp.float32)).astype(jnp.bfloat16)


def occupied_at(occ_ref, row, col):
    high, wide = occ_ref.shape
    inside = (row >= 0) & (row < high) & (col >= 0) & (col < wide)
    value = occ_ref[jnp.clip(row, 0, high - 1), jnp.clip(col, 0, wide - 1)]
    return jnp.where(inside, value, 0)


def row_kernel(
    occ_ref, own_ref, top_ref, bottom_ref, left_ref, right_ref, conv_ref, gain_ref, qkv_ref, out_ref,
    after_ref, grid_s, bias_s, val_s,
):
    rows, length, width = own_ref.shape
    slab, tile = lax.axis_index("slab"), lax.axis_index("tile")
    grid_s[0, REACH : REACH + length] = top_ref[0].astype(jnp.float32)
    grid_s[1 : 1 + rows, REACH : REACH + length] = own_ref[...].astype(jnp.float32)
    grid_s[1 + rows, REACH : REACH + length] = bottom_ref[0].astype(jnp.float32)
    grid_s[:, :REACH] = left_ref[...].astype(jnp.float32)
    grid_s[:, REACH + length :] = right_ref[...].astype(jnp.float32)
    val_s[:, width:] = jnp.ones((val_s.shape[0], width), jnp.bfloat16)
    blocks = length // REACH
    occ_row = slab * rows // BLOCK
    first = tile * (length // BLOCK)
    occ = [occupied_at(occ_ref, occ_row, first - 2 + b) for b in range(2 * blocks + 4)]
    for block in range(blocks):
        bias_s[block] = block_bias(occ[2 * block : 2 * block + 6])
    taps = [[conv_ref[pl.ds(3 * a + b, 1), :] for b in range(3)] for a in range(3)]
    gain = gain_ref[...]
    count = length + 2 * REACH

    def one_row(row, carry):
        above, here, below = grid_s[row], grid_s[row + 1], grid_s[row + 2]
        left, middle, right = (
            taps[0][b] * above + taps[1][b] * here + taps[2][b] * below for b in range(3)
        )
        convolved = here + middle + pltpu.roll(left, 1, 0) + pltpu.roll(right, count - 1, 0)
        stream = convolved.astype(jnp.bfloat16).astype(jnp.float32)
        normed = norm(stream, gain)
        queries = jnp.dot(
            normed[REACH : REACH + length], qkv_ref[:, :width], preferred_element_type=jnp.float32
        )
        queries = (queries * SCALE).astype(jnp.bfloat16)
        key_value = jnp.dot(normed, qkv_ref[:, width:], preferred_element_type=jnp.float32)
        key_value = key_value.astype(jnp.bfloat16)
        keys = key_value[:, :width]
        val_s[:, :width] = key_value[:, width:]
        for block in range(blocks):
            low = block * REACH
            mixture = attend_block(
                queries[low : low + REACH],
                keys[low : low + KEYS],
                val_s[low : low + KEYS],
                bias_s[block],
                occ[2 + 2 * block : 4 + 2 * block],
            )
            update = jnp.dot(mixture, out_ref[...], preferred_element_type=jnp.float32)
            after_ref[row, low : low + REACH] = (
                stream[REACH + low : 2 * REACH + low] + update
            ).astype(jnp.bfloat16)
        return carry

    lax.fori_loop(0, rows, one_row, 0)


def col_kernel(occ_ref, x_ref, gain_ref, qkv_ref, out_ref, mixed_ref, line_s, query_s, key_s, val_s):
    count, width = x_ref.shape
    cols = key_s.shape[0]
    height = count // cols
    slab, tile = lax.axis_index("slab"), lax.axis_index("tile")
    slabs = lax.axis_size("slab")
    occ_col = (tile * slabs + slab) * cols // BLOCK
    line_s[...] = x_ref[...].astype(jnp.float32)
    gain = gain_ref[...]
    for col in range(cols):
        normed = norm(line_s[pl.ds(col, height, stride=cols), :], gain)
        queries = jnp.dot(normed, qkv_ref[:, :width], preferred_element_type=jnp.float32)
        query_s[col] = (queries * SCALE).astype(jnp.bfloat16)
        key_value = jnp.dot(normed, qkv_ref[:, width:], preferred_element_type=jnp.float32)
        key_value = key_value.astype(jnp.bfloat16)
        key_s[col, :REACH] = jnp.zeros((REACH, width), jnp.bfloat16)
        key_s[col, REACH + height :] = jnp.zeros((REACH, width), jnp.bfloat16)
        key_s[col, REACH : REACH + height] = key_value[:, :width]
        val_s[col, :REACH, :width] = jnp.zeros((REACH, width), jnp.bfloat16)
        val_s[col, REACH + height :, :width] = jnp.zeros((REACH, width), jnp.bfloat16)
        val_s[col, REACH : REACH + height, :width] = key_value[:, width:]
        val_s[col, :, width:] = jnp.ones((height + 2 * REACH, width), jnp.bfloat16)

    def one_block(block, carry):
        occ = [occupied_at(occ_ref, 2 * block - 2 + b, occ_col) for b in range(6)]
        bias = block_bias(occ)
        low = pl.multiple_of(block * REACH, REACH)
        for col in range(cols):
            mixture = attend_block(
                query_s[col, pl.ds(low, REACH)],
                key_s[col, pl.ds(low, KEYS)],
                val_s[col, pl.ds(low, KEYS)],
                bias,
                occ[2:4],
            )
            update = jnp.dot(mixture, out_ref[...], preferred_element_type=jnp.float32)
            place = pl.ds(block * (REACH * cols) + col, REACH, stride=cols)
            line_s[place, :] = line_s[place, :] + update
        return carry

    lax.fori_loop(0, height // REACH, one_block, 0)
    mixed_ref[...] = line_s[...].astype(jnp.bfloat16)


VMEM = pl.BlockSpec(memory_space=pltpu.VMEM)
SMEM = pl.BlockSpec(memory_space=pltpu.SMEM)


def exchange(block, axis, dim, width):
    count = lax.axis_size(axis)
    forward = [(i, i + 1) for i in range(count - 1)]
    backward = [(target, source) for source, target in forward]
    extent = block.shape[dim]
    low = lax.ppermute(lax.slice_in_dim(block, extent - width, extent, axis=dim), axis, forward)
    high = lax.ppermute(lax.slice_in_dim(block, 0, width, axis=dim), axis, backward)
    return low, high


def local(tokens, conv_weight, occupancy, row_gain, row_qkv, row_out, col_gain, col_qkv, col_out):
    rows, length, width = tokens.shape
    slabs = lax.axis_size("slab")
    cols = length // slabs
    height = rows * slabs
    count = length + 2 * REACH
    top, bottom = exchange(tokens, "slab", 0, 1)
    left, right = exchange(jnp.concatenate([top, tokens, bottom], axis=0), "tile", 1, REACH)
    after_rows = pl.pallas_call(
        row_kernel,
        out_shape=jax.ShapeDtypeStruct((rows, length, width), jnp.bfloat16),
        in_specs=[SMEM] + [VMEM] * 9,
        out_specs=VMEM,
        scratch_shapes=[
            pltpu.VMEM((rows + 2, count, width), jnp.float32),
            pltpu.VMEM((length // REACH, REACH, KEYS), jnp.float32),
            pltpu.VMEM((count, 2 * width), jnp.bfloat16),
        ],
        name="row_sublayer",
    )(
        occupancy, tokens, top, bottom, left, right,
        conv_weight.reshape(9, width), row_gain.reshape(1, width), row_qkv, row_out,
    )
    columns = lax.all_to_all(after_rows, "slab", split_axis=1, concat_axis=0, tiled=True)
    mixed = pl.pallas_call(
        col_kernel,
        out_shape=jax.ShapeDtypeStruct((height * cols, width), jnp.bfloat16),
        in_specs=[SMEM] + [VMEM] * 4,
        out_specs=VMEM,
        scratch_shapes=[
            pltpu.VMEM((height * cols, width), jnp.float32),
            pltpu.VMEM((cols, height, width), jnp.bfloat16),
            pltpu.VMEM((cols, height + 2 * REACH, width), jnp.bfloat16),
            pltpu.VMEM((cols, height + 2 * REACH, 2 * width), jnp.bfloat16),
        ],
        name="col_sublayer",
    )(occupancy, columns.reshape(height * cols, width), col_gain.reshape(1, width), col_qkv, col_out)
    return mixed.reshape(height, cols, width)


def solution(mesh):
    return jax.shard_map(
        local,
        mesh=mesh,
        in_specs=(P("slab", "tile", None), P(), P(), P(), P(), P(), P(), P(), P()),
        out_specs=P(None, ("tile", "slab"), None),
        check_vma=False,
    )
```

time: 190 us -> 115 us (0.61)
  blocking collectives: 0 us -> 52.4 us
  waiting for transfers between devices: 48.6 us -> 8.85 us
  matrix products: 38.5 us -> 0 us
  Pallas kernels: 0 us -> 32.6 us
  other arithmetic: 26.6 us -> 0 us
  starting transfers between devices: 38 us -> 13.2 us
  local copies, waits for them, and re-layouts: 30.4 us -> 7.18 us
  loops' own time: 6.54 us -> 0 us
    all_to_all x0 -> x1, blocking collectives: none -> 52.4 us  [local(): lax.all_to_all(after_rows, 'slab', split_axis=1, concat_axis=0, tiled=True)]
    all_to_all x1 -> x0, waiting for transfers between devices: 32.8 us -> none  [local(): lax.all_to_all(after_rows, 'slab', split_axis=1, concat_axis=0, tiled=True)]
    pallas_call x0 -> x2, Pallas kernels: none -> 32.6 us  [the longest x1 17.4 us: local(): pl.pallas_call(row_kernel, out_shape=jax.ShapeDtypeStruct((rows, length,...]
    dot_general x22 -> x0, matrix products: 22.9 us -> none  [the longest x16 16.9 us: attend(): jnp.einsum('hqk,khd->qhd', weights, value_heads, preferred_element_type=j...]
    all_to_all x1 -> x0, starting transfers between devices: 19.1 us -> none  [local(): lax.all_to_all(after_rows, 'slab', split_axis=1, concat_axis=0, tiled=True)]
    reduce_sum x4 -> x0, other arithmetic: 17.7 us -> none  [the longest x2 15.4 us: layer_norm(): spread = jnp.mean(centered * centered, axis=-1, keepdims=True)]
    dynamic_slice x71 -> x0, local copies, waits for them, and re-layouts: 17.3 us -> none  [the longest x32 9.88 us: local(): mixture = lax.map(row_attend, (queries, kv_wide, query_ok, key_ok))]
    sub x16 -> x0, matrix products: 15.5 us -> none  [attend(): exp_terms = jnp.exp(scores - row_max)]
  transfers between devices with their start and end apart: 7 -> 4, of which waited for: 4 -> 2; matrix products, arithmetic and copies ran while one was open for 1% -> 2% of each run, Pallas kernels for 0% -> 0%
where the time goes in v1:
time: 115 us; the launch traced here: 114 us
  blocking collectives  52.4 us (46%)
  Pallas kernels  32.6 us (28%)
  starting transfers between devices  13.2 us (11%)
  waiting for transfers between devices  8.85 us (8%)
  local copies, waits for them, and re-layouts  7.18 us (6%)
    all_to_all x1, blocking collectives, local(): lax.all_to_all(after_rows, 'slab', split_axis=1, concat_axis=0, tiled=True)  52.4 us
    pallas_call x1, Pallas kernels, local(): pl.pallas_call(row_kernel, out_shape=jax.ShapeDtypeStruct((rows, length,...  17.4 us
    pallas_call x1, Pallas kernels, local(): pl.pallas_call(col_kernel, out_shape=jax.ShapeDtypeStruct((height * cols,...  15.2 us
    ppermute x2, starting transfers between devices, exchange(): lax.ppermute(lax.slice_in_dim(block, extent - width, extent, axis=dim), a...  6.73 us
    ppermute x2, starting transfers between devices, exchange(): lax.ppermute(lax.slice_in_dim(block, 0, width, axis=dim), axis, backward)  6.44 us
    ppermute x2, waiting for transfers between devices, exchange(): lax.ppermute(lax.slice_in_dim(block, extent - width, extent, axis=dim), a...  4.74 us
    ppermute x2, waiting for transfers between devices, exchange(): lax.ppermute(lax.slice_in_dim(block, 0, width, axis=dim), axis, backward)  4.12 us
    unnamed x12, local copies, waits for them, and re-layouts  3.05 us
  transfers between devices with their start and end apart: 4, of which 2 were waited for; matrix products, arithmetic and copies ran while one was open for 2% of the time, Pallas kernels for 0%

profile of v1, /device:TPU:1, one launch (start us, length us, event | category | flops | bytes accessed | tf_op | source)
XLA Modules:
  0.0 114.3 jit_solution(2128045886599739921)
XLA Ops:
  0.0 0.9 fusion.1
  0.9 4.9 %collective-permute-start = (bf16[1,256,128]{2,1,0:T(8,128)(2,1)S(1)}, bf16[1,256,128]{2,1,0:T(8,128)(2,1)S(1)}, u32[]{:S(2)}, u32[]{:S(2)}) collective-permute-start(bf16[1,256,128]{2,1,0:T(8,128)(2,1)S(1)} %get-tuple-element.8), channel_id=1, source_target_pairs={{0,4},{4,8},{8,12},{12,16},{16,20},{20,24},{24,28},{28,32},{32,36}... | collective-permute-start | bytes 196616 | tf_op jit(solution)/shard_map/ppermute | solution.py:184
  5.8 5.1 %collective-permute-start.1 = (bf16[1,256,128]{2,1,0:T(8,128)(2,1)S(1)}, bf16[1,256,128]{2,1,0:T(8,128)(2,1)S(1)}, u32[]{:S(2)}, u32[]{:S(2)}) collective-permute-start(bf16[1,256,128]{2,1,0:T(8,128)(2,1)S(1)} %get-tuple-element.7), channel_id=1, source_target_pairs={{4,0},{8,4},{12,8},{16,12},{20,16},{24,20},{28,24},{32,28},{36,32}... | collective-permute-start | bytes 196616 | tf_op jit(solution)/shard_map/ppermute | solution.py:185
  11.0 0.0 collective-permute-done.top_ref
  11.0 0.0 copy-start.2
  11.0 0.6 copy-done.2
  11.6 1.1 constant_dynamic-update-slice_fusion.1
  12.7 0.0 collective-permute-done.1.bottom_ref
  12.8 0.0 copy-start.3
  12.8 0.6 copy-done.3
  13.4 0.0 copy-start.4
  13.4 1.8 %collective-permute-start.2 = (bf16[10,128,128]{2,1,0:T(8,128)(2,1)S(1)}, bf16[10,128,128]{2,1,0:T(8,128)(2,1)S(1)}, u32[]{:S(2)}, u32[]{:S(2)}) collective-permute-start(bf16[10,128,128]{2,1,0:T(8,128)(2,1)S(1)} %get-tuple-element.6), channel_id=1, source_target_pairs={{0,1},{1,2},{2,3},{4,5},{5,6},{6,7},{8,9},{9,10},{10,11},{12,13},{... | collective-permute-start | bytes 983048 | tf_op jit(solution)/shard_map/ppermute | solution.py:184
  15.2 1.3 %collective-permute-start.3 = (bf16[10,128,128]{2,1,0:T(8,128)(2,1)S(1)}, bf16[10,128,128]{2,1,0:T(8,128)(2,1)S(1)}, u32[]{:S(2)}, u32[]{:S(2)}) collective-permute-start(bf16[10,128,128]{2,1,0:T(8,128)(2,1)S(1)} %get-tuple-element.5), channel_id=1, source_target_pairs={{1,0},{2,1},{3,2},{5,4},{6,5},{7,6},{9,8},{10,9},{11,10},{13,12},{... | collective-permute-start | bytes 983048 | tf_op jit(solution)/shard_map/ppermute | solution.py:185
  16.5 0.0 copy-done.4
  16.5 0.6 reshape.16.conv_ref
  17.1 4.7 %collective-permute-done.2.left_ref = bf16[10,128,128]{2,1,0:T(8,128)(2,1)S(1)} collective-permute-done((bf16[10,128,128]{2,1,0:T(8,128)(2,1)S(1)}, bf16[10,128,128]{2,1,0:T(8,128)(2,1)S(1)}, u32[]{:S(2)}, u32[]{:S(2)}) %collective-permute-start.2) | collective-permute-done | bytes 327712 | tf_op jit(solution)/shard_map/ppermute | solution.py:184
  21.9 0.0 copy-start
  21.9 4.1 %collective-permute-done.3.right_ref = bf16[10,128,128]{2,1,0:T(8,128)(2,1)S(1)} collective-permute-done((bf16[10,128,128]{2,1,0:T(8,128)(2,1)S(1)}, bf16[10,128,128]{2,1,0:T(8,128)(2,1)S(1)}, u32[]{:S(2)}, u32[]{:S(2)}) %collective-permute-start.3) | collective-permute-done | bytes 327712 | tf_op jit(solution)/shard_map/ppermute | solution.py:185
  26.0 0.0 copy-start.1
  26.0 0.0 copy-done
  26.0 0.7 copy-done.1
  26.7 17.4 %row_sublayer.1 = bf16[8,256,128]{2,1,0:T(8,128)(2,1)} custom-call(s32[16,16]{1,0:T(8,128)} %occ_ref.3, bf16[8,256,128]{2,1,0:T(8,128)(2,1)} %own_ref.1, bf16[1,256,128]{2,1,0:T(8,128)(2,1)} %copy-done.2, bf16[1,256,128]{2,1,0:T(8,128)(2,1)} %copy-done.3, bf16[10,128,128]{2,1,0:T(8,128)(2,1)} %copy-done, bf16[10,128,128]{2,1,0:T(8,128)(2,1)} %copy-done.1, ...), custom_call_target="tpu_custom_call" | custom-call | tf_op jit(solution)/shard_map/row_sublayer/pallas_call | solution.py:197
  44.1 1.4 %copy.11 = bf16[8,256,128]{2,0,1:T(8,128)(2,1)S(1)} copy(bf16[8,256,128]{2,1,0:T(8,128)(2,1)} %row_sublayer.1) | data formatting | bytes 1048576 | tf_op jit(solution)/shard_map/row_sublayer/pallas_call | solution.py:197
  45.5 52.4 %all_to_all.15 = bf16[8,256,128]{2,0,1:T(8,128)(2,1)S(1)} all-to-all(bf16[8,256,128]{2,0,1:T(8,128)(2,1)S(1)} %copy.11), channel_id=1, replica_groups=mesh['slab'=128,'tile'=4] {'slab'}, dimensions={1} | all-to-all | bytes 1048576 | tf_op jit(solution)/shard_map/all_to_all | solution.py:212
  97.9 1.2 %copy.12 = bf16[8,128,2,128]{3,2,0,1:T(2,128)(2,1)} copy(bf16[8,128,2,128]{3,0,2,1:T(8,128)(2,1)S(1)} %bitcast.7) | data formatting | bytes 1048576 | tf_op jit(solution)/shard_map/all_to_all | solution.py:212
  99.1 15.2 %col_sublayer.1 = bf16[2048,128]{1,0:T(8,128)(2,1)} custom-call(s32[16,16]{1,0:T(8,128)} %occ_ref.3, bf16[2048,128]{1,0:T(8,128)(2,1)} %bitcast.8, f32[1,128]{1,0:T(1,128)} %bitcast.10, bf16[128,384]{1,0:T(8,128)(2,1)} %qkv_ref.3, bf16[128,128]{1,0:T(8,128)(2,1)} %out_ref.3), custom_call_target="tpu_custom_call" | custom-call | tf_op jit(solution)/shard_map/col_sublayer/pallas_call | solution.py:213
  (3 shorter events, 0.1 us)
Async XLA Ops:
  0.9 10.1 %collective-permute-start = (bf16[1,256,128]{2,1,0:T(8,128)(2,1)S(1)}, bf16[1,256,128]{2,1,0:T(8,128)(2,1)S(1)}, u32[]{:S(2)}, u32[]{:S(2)}) collective-permute-start(bf16[1,256,128]{2,1,0:T(8,128)(2,1)S(1)} %get-tuple-element.8), channel_id=1, source_target_pairs={{0,4},{4,8},{8,12},{12,16},{16,20},{20,24},{24,28},{28,32},{32,36}... | collective-permute-start | bytes 196616 | tf_op jit(solution)/shard_map/ppermute | solution.py:184
  5.8 6.9 %collective-permute-start.1 = (bf16[1,256,128]{2,1,0:T(8,128)(2,1)S(1)}, bf16[1,256,128]{2,1,0:T(8,128)(2,1)S(1)}, u32[]{:S(2)}, u32[]{:S(2)}) collective-permute-start(bf16[1,256,128]{2,1,0:T(8,128)(2,1)S(1)} %get-tuple-element.7), channel_id=1, source_target_pairs={{4,0},{8,4},{12,8},{16,12},{20,16},{24,20},{28,24},{32,28},{36,32}... | collective-permute-start | bytes 196616 | tf_op jit(solution)/shard_map/ppermute | solution.py:185
  11.0 0.6 copy-start.2
  12.8 0.6 copy-start.3
  13.4 3.2 %copy-start.4 = (f32[3,3,128]{2,1,0:T(4,128)S(1)}, f32[3,3,128]{2,1,0:T(4,128)}, u32[]{:S(2)}) copy-start(f32[3,3,128]{2,1,0:T(4,128)} %param.10) | copy-start | bytes 13828
  13.4 8.5 %collective-permute-start.2 = (bf16[10,128,128]{2,1,0:T(8,128)(2,1)S(1)}, bf16[10,128,128]{2,1,0:T(8,128)(2,1)S(1)}, u32[]{:S(2)}, u32[]{:S(2)}) collective-permute-start(bf16[10,128,128]{2,1,0:T(8,128)(2,1)S(1)} %get-tuple-element.6), channel_id=1, source_target_pairs={{0,1},{1,2},{2,3},{4,5},{5,6},{6,7},{8,9},{9,10},{10,11},{12,13},{... | collective-permute-start | bytes 983048 | tf_op jit(solution)/shard_map/ppermute | solution.py:184
  15.2 10.8 %collective-permute-start.3 = (bf16[10,128,128]{2,1,0:T(8,128)(2,1)S(1)}, bf16[10,128,128]{2,1,0:T(8,128)(2,1)S(1)}, u32[]{:S(2)}, u32[]{:S(2)}) collective-permute-start(bf16[10,128,128]{2,1,0:T(8,128)(2,1)S(1)} %get-tuple-element.5), channel_id=1, source_target_pairs={{1,0},{2,1},{3,2},{5,4},{6,5},{7,6},{9,8},{10,9},{11,10},{13,12},{... | collective-permute-start | bytes 983048 | tf_op jit(solution)/shard_map/ppermute | solution.py:185
  21.9 4.1 %copy-start = (bf16[10,128,128]{2,1,0:T(8,128)(2,1)}, bf16[10,128,128]{2,1,0:T(8,128)(2,1)S(1)}, u32[]{:S(2)}) copy-start(bf16[10,128,128]{2,1,0:T(8,128)(2,1)S(1)} %collective-permute-done.2.left_ref) | copy-start | bytes 983044
  26.0 0.7 copy-start.1

commit v2 on v1

--- a/solution.py
+++ b/solution.py
@@ -1,3 +1,4 @@
+import functools
 import math
 
 import jax
@@ -83,6 +84,24 @@
     grid_s[1 + rows, REACH : REACH + length] = bottom_ref[0].astype(jnp.float32)
     grid_s[:, :REACH] = left_ref[...].astype(jnp.float32)
     grid_s[:, REACH + length :] = right_ref[...].astype(jnp.float32)
+    nothing = jnp.zeros((rows + 2, REACH, width), jnp.float32)
+
+    @pl.when(slab == 0)
+    def _():
+        grid_s[0] = jnp.zeros(grid_s.shape[1:], jnp.float32)
+
+    @pl.when(slab == lax.axis_size("slab") - 1)
+    def _():
+        grid_s[1 + rows] = jnp.zeros(grid_s.shape[1:], jnp.float32)
+
+    @pl.when(tile == 0)
+    def _():
+        grid_s[:, :REACH] = nothing
+
+    @pl.when(tile == lax.axis_size("tile") - 1)
+    def _():
+        grid_s[:, REACH + length :] = nothing
+
     val_s[:, width:] = jnp.ones((val_s.shape[0], width), jnp.bfloat16)
     blocks = length // REACH
     occ_row = slab * rows // BLOCK
@@ -176,14 +195,80 @@
 SMEM = pl.BlockSpec(memory_space=pltpu.SMEM)
 
 
-def exchange(block, axis, dim, width):
-    count = lax.axis_size(axis)
-    forward = [(i, i + 1) for i in range(count - 1)]
-    backward = [(target, source) for source, target in forward]
-    extent = block.shape[dim]
-    low = lax.ppermute(lax.slice_in_dim(block, extent - width, extent, axis=dim), axis, forward)
-    high = lax.ppermute(lax.slice_in_dim(block, 0, width, axis=dim), axis, backward)
-    return low, high
+ANY = pl.BlockSpec(memory_space=pl.ANY)
+MESH = pl.DeviceIdType.MESH
+
+
+def halo_kernel(own_ref, top_ref, bottom_ref, left_ref, right_ref, send_sem, recv_sem):
+    rows, length, width = own_ref.shape
+    slabs, tiles = lax.axis_size("slab"), lax.axis_size("tile")
+    slab, tile = lax.axis_index("slab"), lax.axis_index("tile")
+    down, up = lax.rem(slab + 1, slabs), lax.rem(slab + slabs - 1, slabs)
+    east, west = lax.rem(tile + 1, tiles), lax.rem(tile + tiles - 1, tiles)
+    low, high = pl.ds(0, REACH), pl.ds(length - REACH, REACH)
+    first, last, inner = pl.ds(0, 1), pl.ds(rows - 1, 1), pl.ds(1, rows)
+    after = pl.ds(rows + 1, 1)
+    plan = [
+        (own_ref.at[:, high], left_ref.at[inner], (slab, east)),
+        (own_ref.at[:, low], right_ref.at[inner], (slab, west)),
+        (own_ref.at[last, high], left_ref.at[first], (down, east)),
+        (own_ref.at[last, low], right_ref.at[first], (down, west)),
+        (own_ref.at[first, high], left_ref.at[after], (up, east)),
+        (own_ref.at[first, low], right_ref.at[after], (up, west)),
+        (own_ref.at[last], top_ref, (down, tile)),
+        (own_ref.at[first], bottom_ref, (up, tile)),
+    ]
+    barrier = pltpu.get_barrier_semaphore()
+    for _, _, device in plan:
+        pl.semaphore_signal(barrier, inc=1, device_id=device, device_id_type=MESH)
+    pl.semaphore_wait(barrier, len(plan))
+    copies = [
+        pltpu.make_async_remote_copy(
+            src_ref=source, dst_ref=target, send_sem=send_sem.at[k], recv_sem=recv_sem.at[k],
+            device_id=device, device_id_type=MESH,
+        )
+        for k, (source, target, device) in enumerate(plan)
+    ]
+    for copy in copies:
+        copy.start()
+    for copy in copies:
+        copy.wait()
+
+
+def swap_kernel(slabs, after_ref, columns_ref, own_sem, send_sem, recv_sem):
+    rows = after_ref.shape[0]
+    slab, tile = lax.axis_index("slab"), lax.axis_index("tile")
+    barrier = pltpu.get_barrier_semaphore()
+
+    def greet(k, carry):
+        device = (lax.rem(slab + k, slabs), tile)
+        pl.semaphore_signal(barrier, inc=1, device_id=device, device_id_type=MESH)
+        return carry
+
+    lax.fori_loop(1, slabs, greet, 0)
+    place = pl.ds(slab * rows, rows)
+    own = pltpu.make_async_copy(after_ref.at[:, slab], columns_ref.at[place], own_sem)
+    own.start()
+    pl.semaphore_wait(barrier, slabs - 1)
+
+    def send(k, carry):
+        step = (k + 1) // 2
+        to = lax.rem(slab + lax.rem(k, 2) * step + (1 - lax.rem(k, 2)) * (slabs - step), slabs)
+        pltpu.make_async_remote_copy(
+            src_ref=after_ref.at[:, to], dst_ref=columns_ref.at[place],
+            send_sem=send_sem, recv_sem=recv_sem, device_id=(to, tile), device_id_type=MESH,
+        ).start()
+        return carry
+
+    lax.fori_loop(1, slabs, send, 0)
+    own.wait()
+    sent = columns_ref.at[pl.ds(0, (slabs - 1) * rows)]
+    whole = pltpu.make_async_remote_copy(
+        src_ref=sent, dst_ref=sent, send_sem=send_sem, recv_sem=recv_sem,
+        device_id=(lax.rem(slab + 1, slabs), tile), device_id_type=MESH,
+    )
+    whole.wait_send()
+    whole.wait_recv()
 
 
 def local(tokens, conv_weight, occupancy, row_gain, row_qkv, row_out, col_gain, col_qkv, col_out):
@@ -192,8 +277,17 @@
     cols = length // slabs
     height = rows * slabs
     count = length + 2 * REACH
-    top, bottom = exchange(tokens, "slab", 0, 1)
-    left, right = exchange(jnp.concatenate([top, tokens, bottom], axis=0), "tile", 1, REACH)
+    edge = jax.ShapeDtypeStruct((1, length, width), tokens.dtype)
+    side = jax.ShapeDtypeStruct((rows + 2, REACH, width), tokens.dtype)
+    top, bottom, left, right = pl.pallas_call(
+        halo_kernel,
+        out_shape=(edge, edge, side, side),
+        in_specs=[ANY],
+        out_specs=(ANY,) * 4,
+        scratch_shapes=[pltpu.SemaphoreType.DMA((8,)), pltpu.SemaphoreType.DMA((8,))],
+        compiler_params=pltpu.CompilerParams(collective_id=0, has_side_effects=True),
+        name="halo",
+    )(tokens)
     after_rows = pl.pallas_call(
         row_kernel,
         out_shape=jax.ShapeDtypeStruct((rows, length, width), jnp.bfloat16),
@@ -209,7 +303,15 @@
         occupancy, tokens, top, bottom, left, right,
         conv_weight.reshape(9, width), row_gain.reshape(1, width), row_qkv, row_out,
     )
-    columns = lax.all_to_all(after_rows, "slab", split_axis=1, concat_axis=0, tiled=True)
+    columns = pl.pallas_call(
+        functools.partial(swap_kernel, slabs),
+        out_shape=jax.ShapeDtypeStruct((height, cols, width), jnp.bfloat16),
+        in_specs=[VMEM],
+        out_specs=ANY,
+        scratch_shapes=[pltpu.SemaphoreType.DMA] * 3,
+        compiler_params=pltpu.CompilerParams(collective_id=1, has_side_effects=True),
+        name="swap",
+    )(after_rows.reshape(rows, slabs, cols, width))
     mixed = pl.pallas_call(
         col_kernel,
         out_shape=jax.ShapeDtypeStruct((height * cols, width), jnp.bfloat16),

time: 115 us -> 93.5 us (0.81)
  Pallas kernels: 32.6 us -> 91.9 us
  blocking collectives: 52.4 us -> 0 us
  starting transfers between devices: 13.2 us -> 0 us
  waiting for transfers between devices: 8.85 us -> 0 us
  local copies, waits for them, and re-layouts: 7.18 us -> 1.29 us
    pallas_call x0 -> x2, Pallas kernels: none -> 59.2 us  [the longest x1 38.1 us: local(): pl.pallas_call(functools.partial(swap_kernel, slabs), out_shape=jax.Shape...]
    all_to_all x1 -> x0, blocking collectives: 52.4 us -> none  [local(): lax.all_to_all(after_rows, 'slab', split_axis=1, concat_axis=0, tiled=True)]
    ppermute x4 -> x0, starting transfers between devices: 13.2 us -> none  [the longest x2 6.73 us: exchange(): lax.ppermute(lax.slice_in_dim(block, extent - width, extent, axis=dim), a...]
    ppermute x4 -> x0, waiting for transfers between devices: 8.85 us -> none  [the longest x2 4.74 us: exchange(): lax.ppermute(lax.slice_in_dim(block, extent - width, extent, axis=dim), a...]
    unnamed x12 -> x0, local copies, waits for them, and re-layouts: 3.05 us -> none
    pallas_call x1 -> x0, local copies, waits for them, and re-layouts: 1.38 us -> none  [local(): pl.pallas_call(row_kernel, out_shape=jax.ShapeDtypeStruct((rows, length,...]
    all_to_all x1 -> x0, local copies, waits for them, and re-layouts: 1.21 us -> none  [local(): lax.all_to_all(after_rows, 'slab', split_axis=1, concat_axis=0, tiled=True)]
  transfers between devices with their start and end apart: 4 -> 0, of which waited for: 2 -> 0; matrix products, arithmetic and copies ran while one was open for 2% -> 0% of each run, Pallas kernels for 0% -> 0%
where the time goes in v2:
time: 93.5 us; the launch traced here: 93.2 us
  Pallas kernels  91.9 us (98%)
  local copies, waits for them, and re-layouts  1.29 us (1%)
    pallas_call x1, Pallas kernels, local(): pl.pallas_call(functools.partial(swap_kernel, slabs), out_shape=jax.Shape...  38.1 us
    pallas_call x1, Pallas kernels, local(): pl.pallas_call(halo_kernel, out_shape=(edge, edge, side, side), in_specs=...  21.1 us
    pallas_call x1, Pallas kernels, local(): pl.pallas_call(row_kernel, out_shape=jax.ShapeDtypeStruct((rows, length,...  17.4 us
    pallas_call x1, Pallas kernels, local(): pl.pallas_call(col_kernel, out_shape=jax.ShapeDtypeStruct((height * cols,...  15.2 us

profile of v2, /device:TPU:1, one launch (start us, length us, event | category | flops | bytes accessed | tf_op | source)
XLA Modules:
  0.0 93.2 jit_solution(5773042005216760690)
XLA Ops:
  0.0 1.3 %reshape.18.conv_ref = f32[9,128]{1,0:T(8,128)} reshape(f32[3,3,128]{2,1,0:T(4,128)} %param.10) | data formatting | bytes 9216 | tf_op jit(solution)/shard_map/reshape | solution.py:304
  1.3 21.1 %halo.1 = (bf16[1,256,128]{2,1,0:T(8,128)(2,1)}, bf16[1,256,128]{2,1,0:T(8,128)(2,1)}, bf16[10,128,128]{2,1,0:T(8,128)(2,1)}, bf16[10,128,128]{2,1,0:T(8,128)(2,1)}) custom-call(bf16[8,256,128]{2,1,0:T(8,128)(2,1)} %own_ref.3), custom_call_target="tpu_custom_call" | custom-call | tf_op jit(solution)/shard_map/halo/pallas_call | solution.py:282
  22.4 17.4 %row_sublayer.1 = bf16[8,256,128]{2,1,0:T(8,128)(2,1)} custom-call(s32[16,16]{1,0:T(8,128)} %occ_ref.3, bf16[8,256,128]{2,1,0:T(8,128)(2,1)} %own_ref.3, bf16[1,256,128]{2,1,0:T(8,128)(2,1)} %get-tuple-element.9.top_ref, bf16[1,256,128]{2,1,0:T(8,128)(2,1)} %get-tuple-element.10.bottom_ref, bf16[10,128,128]{2,1,0:T(8,128)(2,1)} %get-tuple-element.11.left_ref, ...), custom_call_target="tpu_custom_call" | custom-call | tf_op jit(solution)/shard_map/row_sublayer/pallas_call | solution.py:291
  39.8 38.1 %swap.1 = bf16[1024,2,128]{2,1,0:T(2,128)(2,1)} custom-call(bf16[8,128,2,128]{3,2,1,0:T(2,128)(2,1)} %bitcast.5), custom_call_target="tpu_custom_call" | custom-call | tf_op jit(solution)/shard_map/swap/pallas_call | solution.py:306
  78.0 15.2 %col_sublayer.1 = bf16[2048,128]{1,0:T(8,128)(2,1)} custom-call(s32[16,16]{1,0:T(8,128)} %occ_ref.3, bf16[2048,128]{1,0:T(8,128)(2,1)} %bitcast.6, f32[1,128]{1,0:T(1,128)} %bitcast.8, bf16[128,384]{1,0:T(8,128)(2,1)} %qkv_ref.3, bf16[128,128]{1,0:T(8,128)(2,1)} %out_ref.3), custom_call_target="tpu_custom_call" | custom-call | tf_op jit(solution)/shard_map/col_sublayer/pallas_call | solution.py:315

commit v3 on v2

--- a/solution.py
+++ b/solution.py
@@ -1,4 +1,3 @@
-import functools
 import math
 
 import jax
@@ -13,6 +12,7 @@
 BLOCK = 64
 REACH = 128
 KEYS = 3 * REACH
+GROUP = 4
 NEG = -1e30
 SCALE = math.log2(math.e) / math.sqrt(HEAD_DIM)
 
@@ -75,10 +75,19 @@
 
 def row_kernel(
     occ_ref, own_ref, top_ref, bottom_ref, left_ref, right_ref, conv_ref, gain_ref, qkv_ref, out_ref,
-    after_ref, grid_s, bias_s, val_s,
+    columns_ref, grid_s, bias_s, val_s, after_s, own_sem, send_sem, recv_sem,
 ):
     rows, length, width = own_ref.shape
+    slabs, cols = after_s.shape[1:3]
     slab, tile = lax.axis_index("slab"), lax.axis_index("tile")
+    barrier = pltpu.get_barrier_semaphore()
+
+    def greet(k, carry):
+        device = (lax.rem(slab + k, slabs), tile)
+        pl.semaphore_signal(barrier, inc=1, device_id=device, device_id_type=MESH)
+        return carry
+
+    lax.fori_loop(1, slabs, greet, 0)
     grid_s[0, REACH : REACH + length] = top_ref[0].astype(jnp.float32)
     grid_s[1 : 1 + rows, REACH : REACH + length] = own_ref[...].astype(jnp.float32)
     grid_s[1 + rows, REACH : REACH + length] = bottom_ref[0].astype(jnp.float32)
@@ -139,12 +148,47 @@
                 occ[2 + 2 * block : 4 + 2 * block],
             )
             update = jnp.dot(mixture, out_ref[...], preferred_element_type=jnp.float32)
-            after_ref[row, low : low + REACH] = (
-                stream[REACH + low : 2 * REACH + low] + update
+            result = stream[REACH + low : 2 * REACH + low] + update
+            after_s[row, low // cols : (low + REACH) // cols] = result.reshape(
+                REACH // cols, cols, width
             ).astype(jnp.bfloat16)
         return carry
 
-    lax.fori_loop(0, rows, one_row, 0)
+    for group in range(rows // GROUP):
+        start = group * GROUP
+        lax.fori_loop(start, start + GROUP, one_row, 0)
+        if group == 0:
+            pl.semaphore_wait(barrier, slabs - 1)
+        taken = pl.ds(start, GROUP)
+        place = pl.ds(slab * rows + start, GROUP)
+        pltpu.make_async_copy(
+            after_s.at[taken, slab], columns_ref.at[place], own_sem.at[group]
+        ).start()
+
+        def send(k, carry):
+            step = (k + 1) // 2
+            to = lax.rem(slab + lax.rem(k, 2) * step + (1 - lax.rem(k, 2)) * (slabs - step), slabs)
+            pltpu.make_async_remote_copy(
+                src_ref=after_s.at[taken, to], dst_ref=columns_ref.at[place],
+                send_sem=send_sem, recv_sem=recv_sem, device_id=(to, tile), device_id_type=MESH,
+            ).start()
+            return carry
+
+        lax.fori_loop(1, slabs, send, 0)
+    for group in range(rows // GROUP):
+        start = group * GROUP
+        pltpu.make_async_copy(
+            after_s.at[pl.ds(start, GROUP), slab],
+            columns_ref.at[pl.ds(slab * rows + start, GROUP)],
+            own_sem.at[group],
+        ).wait()
+    sent = columns_ref.at[pl.ds(0, (slabs - 1) * rows)]
+    whole = pltpu.make_async_remote_copy(
+        src_ref=sent, dst_ref=sent, send_sem=send_sem, recv_sem=recv_sem,
+        device_id=(lax.rem(slab + 1, slabs), tile), device_id_type=MESH,
+    )
+    whole.wait_send()
+    whole.wait_recv()
 
 
 def col_kernel(occ_ref, x_ref, gain_ref, qkv_ref, out_ref, mixed_ref, line_s, query_s, key_s, val_s):
@@ -235,42 +279,6 @@
         copy.wait()
 
 
-def swap_kernel(slabs, after_ref, columns_ref, own_sem, send_sem, recv_sem):
-    rows = after_ref.shape[0]
-    slab, tile = lax.axis_index("slab"), lax.axis_index("tile")
-    barrier = pltpu.get_barrier_semaphore()
-
-    def greet(k, carry):
-        device = (lax.rem(slab + k, slabs), tile)
-        pl.semaphore_signal(barrier, inc=1, device_id=device, device_id_type=MESH)
-        return carry
-
-    lax.fori_loop(1, slabs, greet, 0)
-    place = pl.ds(slab * rows, rows)
-    own = pltpu.make_async_copy(after_ref.at[:, slab], columns_ref.at[place], own_sem)
-    own.start()
-    pl.semaphore_wait(barrier, slabs - 1)
-
-    def send(k, carry):
-        step = (k + 1) // 2
-        to = lax.rem(slab + lax.rem(k, 2) * step + (1 - lax.rem(k, 2)) * (slabs - step), slabs)
-        pltpu.make_async_remote_copy(
-            src_ref=after_ref.at[:, to], dst_ref=columns_ref.at[place],
-            send_sem=send_sem, recv_sem=recv_sem, device_id=(to, tile), device_id_type=MESH,
-        ).start()
-        return carry
-
-    lax.fori_loop(1, slabs, send, 0)
-    own.wait()
-    sent = columns_ref.at[pl.ds(0, (slabs - 1) * rows)]
-    whole = pltpu.make_async_remote_copy(
-        src_ref=sent, dst_ref=sent, send_sem=send_sem, recv_sem=recv_sem,
-        device_id=(lax.rem(slab + 1, slabs), tile), device_id_type=MESH,
-    )
-    whole.wait_send()
-    whole.wait_recv()
-
-
 def local(tokens, conv_weight, occupancy, row_gain, row_qkv, row_out, col_gain, col_qkv, col_out):
     rows, length, width = tokens.shape
     slabs = lax.axis_size("slab")
@@ -288,30 +296,26 @@
         compiler_params=pltpu.CompilerParams(collective_id=0, has_side_effects=True),
         name="halo",
     )(tokens)
-    after_rows = pl.pallas_call(
+    columns = pl.pallas_call(
         row_kernel,
-        out_shape=jax.ShapeDtypeStruct((rows, length, width), jnp.bfloat16),
+        out_shape=jax.ShapeDtypeStruct((height, cols, width), jnp.bfloat16),
         in_specs=[SMEM] + [VMEM] * 9,
-        out_specs=VMEM,
+        out_specs=ANY,
         scratch_shapes=[
             pltpu.VMEM((rows + 2, count, width), jnp.float32),
             pltpu.VMEM((length // REACH, REACH, KEYS), jnp.float32),
             pltpu.VMEM((count, 2 * width), jnp.bfloat16),
+            pltpu.VMEM((rows, slabs, cols, width), jnp.bfloat16),
+            pltpu.SemaphoreType.DMA((rows // GROUP,)),
+            pltpu.SemaphoreType.DMA,
+            pltpu.SemaphoreType.DMA,
         ],
+        compiler_params=pltpu.CompilerParams(collective_id=1, has_side_effects=True),
         name="row_sublayer",
     )(
         occupancy, tokens, top, bottom, left, right,
         conv_weight.reshape(9, width), row_gain.reshape(1, width), row_qkv, row_out,
     )
-    columns = pl.pallas_call(
-        functools.partial(swap_kernel, slabs),
-        out_shape=jax.ShapeDtypeStruct((height, cols, width), jnp.bfloat16),
-        in_specs=[VMEM],
-        out_specs=ANY,
-        scratch_shapes=[pltpu.SemaphoreType.DMA] * 3,
-        compiler_params=pltpu.CompilerParams(collective_id=1, has_side_effects=True),
-        name="swap",
-    )(after_rows.reshape(rows, slabs, cols, width))
     mixed = pl.pallas_call(
         col_kernel,
         out_shape=jax.ShapeDtypeStruct((height * cols, width), jnp.bfloat16),

time: 93.5 us -> 81 us (0.87)
  Pallas kernels: 91.9 us -> 79.5 us
    pallas_call x2 -> x1, Pallas kernels: 55.5 us -> 43.1 us  [local(): pl.pallas_call(row_kernel, out_shape=jax.ShapeDtypeStruct((height, cols,...]
where the time goes in v3:
time: 81 us; the launch traced here: 80.8 us
  Pallas kernels  79.5 us (98%)
  local copies, waits for them, and re-layouts  1.3 us (2%)
    pallas_call x1, Pallas kernels, local(): pl.pallas_call(row_kernel, out_shape=jax.ShapeDtypeStruct((height, cols,...  43.1 us
    pallas_call x1, Pallas kernels, local(): pl.pallas_call(halo_kernel, out_shape=(edge, edge, side, side), in_specs=...  21.1 us
    pallas_call x1, Pallas kernels, local(): pl.pallas_call(col_kernel, out_shape=jax.ShapeDtypeStruct((height * cols,...  15.2 us

profile of v3, /device:TPU:1, one launch (start us, length us, event | category | flops | bytes accessed | tf_op | source)
XLA Modules:
  0.0 80.8 jit_solution(4592375597687866614)
XLA Ops:
  0.0 1.3 %reshape.15.conv_ref = f32[9,128]{1,0:T(8,128)} reshape(f32[3,3,128]{2,1,0:T(4,128)} %param.10) | data formatting | bytes 9216 | tf_op jit(solution)/shard_map/reshape | solution.py:317
  1.3 21.1 %halo.1 = (bf16[1,256,128]{2,1,0:T(8,128)(2,1)}, bf16[1,256,128]{2,1,0:T(8,128)(2,1)}, bf16[10,128,128]{2,1,0:T(8,128)(2,1)}, bf16[10,128,128]{2,1,0:T(8,128)(2,1)}) custom-call(bf16[8,256,128]{2,1,0:T(8,128)(2,1)} %own_ref.3), custom_call_target="tpu_custom_call" | custom-call | tf_op jit(solution)/shard_map/halo/pallas_call | solution.py:290
  22.4 43.1 %row_sublayer.1 = bf16[1024,2,128]{2,1,0:T(2,128)(2,1)} custom-call(s32[16,16]{1,0:T(8,128)} %occ_ref.3, bf16[8,256,128]{2,1,0:T(8,128)(2,1)} %own_ref.3, bf16[1,256,128]{2,1,0:T(8,128)(2,1)} %get-tuple-element.9.top_ref, bf16[1,256,128]{2,1,0:T(8,128)(2,1)} %get-tuple-element.10.bottom_ref, bf16[10,128,128]{2,1,0:T(8,128)(2,1)} %get-tuple-element.11.left_ref, ...), custom_call_target="tpu_custom_call" | custom-call | tf_op jit(solution)/shard_map/row_sublayer/pallas_call | solution.py:299
  65.6 15.2 %col_sublayer.1 = bf16[2048,128]{1,0:T(8,128)(2,1)} custom-call(s32[16,16]{1,0:T(8,128)} %occ_ref.3, bf16[2048,128]{1,0:T(8,128)(2,1)} %bitcast.4, f32[1,128]{1,0:T(1,128)} %bitcast.6, bf16[128,384]{1,0:T(8,128)(2,1)} %qkv_ref.3, bf16[128,128]{1,0:T(8,128)(2,1)} %out_ref.3), custom_call_target="tpu_custom_call" | custom-call | tf_op jit(solution)/shard_map/col_sublayer/pallas_call | solution.py:319

commit v4 on v3

--- a/solution.py
+++ b/solution.py
@@ -25,45 +25,47 @@
 
 
 def block_bias(key_occupied):
-    lane = lax.broadcasted_iota(jnp.int32, (1, KEYS), 1) // BLOCK
-    key_bias = jnp.zeros((1, KEYS), jnp.float32)
+    at = lax.broadcasted_iota(jnp.int32, (KEYS, REACH), 0)
+    key_bias = jnp.zeros((KEYS, REACH), jnp.float32)
     for index, occupied in enumerate(key_occupied):
         value = jnp.where(occupied > 0, jnp.float32(0.0), jnp.float32(NEG))
-        key_bias = jnp.where(lane == index, value, key_bias)
-    query = lax.broadcasted_iota(jnp.int32, (REACH, KEYS), 0)
-    key = lax.broadcasted_iota(jnp.int32, (REACH, KEYS), 1) - REACH
-    offset = query - key
-    bias = jnp.where(jnp.abs(offset) < REACH, jnp.broadcast_to(key_bias, offset.shape), NEG)
+        key_bias = jnp.where(at // BLOCK == index, value, key_bias)
+    offset = lax.broadcasted_iota(jnp.int32, (KEYS, REACH), 1) - (at - REACH)
+    bias = jnp.where(jnp.abs(offset) < REACH, key_bias, NEG)
     return jnp.where(offset == 0, 0.0, bias)
 
 
-def heads_of(lane_shape):
-    return lax.broadcasted_iota(jnp.int32, lane_shape, 1) // HEAD_DIM
-
-
-def attend_block(queries, keys, values_ones, bias, query_occupied):
-    head = heads_of((REACH, 128))
+def attend_block(queries, keys, values_t, bias, query_occupied, out_weight):
+    head = lax.broadcasted_iota(jnp.int32, (REACH, 128), 1) // HEAD_DIM
     zero = jnp.zeros_like(queries)
     stacked = jnp.concatenate([jnp.where(head == h, queries, zero) for h in range(HEADS)], axis=0)
     scores = lax.dot_general(
-        stacked, keys, (((1,), (1,)), ((), ())), preferred_element_type=jnp.float32
-    )
-    parts = []
+        keys, stacked, (((1,), (1,)), ((), ())), preferred_element_type=jnp.float32
+    )
+    lane = lax.broadcasted_iota(jnp.int32, (1, REACH), 1)
+    occupied = jnp.where(lane < BLOCK, query_occupied[0], query_occupied[1]).astype(jnp.float32)
+    mixtures = []
     for h in range(HEADS):
-        part = scores[h * REACH : (h + 1) * REACH] + bias
-        top = jnp.max(part, axis=-1, keepdims=True)
-        parts.append(jnp.exp2(part - top).astype(jnp.bfloat16))
-    weights = jnp.concatenate(parts, axis=0)
-    both = jnp.dot(weights, values_ones, preferred_element_type=jnp.float32)
-    mixture, total = both[:REACH, :128], both[:REACH, 128:]
-    for h in range(1, HEADS):
-        rows = both[h * REACH : (h + 1) * REACH]
-        mixture = jnp.where(head == h, rows[:, :128], mixture)
-        total = jnp.where(head == h, rows[:, 128:], total)
-    mixture = mixture / total
-    row = lax.broadcasted_iota(jnp.int32, (REACH, 128), 0)
-    occupied = jnp.where(row < BLOCK, query_occupied[0], query_occupied[1])
-    return (mixture * occupied.astype(jnp.float32)).astype(jnp.bfloat16)
+        part = scores[:, h * REACH : (h + 1) * REACH] + bias
+        weights = jnp.exp2(part - jnp.max(part, axis=0, keepdims=True))
+        total = jnp.sum(weights, axis=0, keepdims=True)
+        mixture = jnp.dot(
+            values_t[h * HEAD_DIM : (h + 1) * HEAD_DIM],
+            weights.astype(jnp.bfloat16),
+            preferred_element_type=jnp.float32,
+        )
+        mixtures.append(mixture * (occupied / total))
+    mixture = jnp.concatenate(mixtures, axis=0).T.astype(jnp.bfloat16)
+    return jnp.dot(mixture, out_weight, preferred_element_type=jnp.float32)
+
+
+def project(normed, qkv_ref, width):
+    both = jnp.dot(normed, qkv_ref[:, : 2 * width], preferred_element_type=jnp.float32)
+    values_t = lax.dot_general(
+        qkv_ref[:, 2 * width :], normed, (((0,), (1,)), ((), ())), preferred_element_type=jnp.float32
+    )
+    queries = (both[:, :width] * SCALE).astype(jnp.bfloat16)
+    return queries, both[:, width:].astype(jnp.bfloat16), values_t.astype(jnp.bfloat16)
 
 
 def occupied_at(occ_ref, row, col):
@@ -75,7 +77,7 @@
 
 def row_kernel(
     occ_ref, own_ref, top_ref, bottom_ref, left_ref, right_ref, conv_ref, gain_ref, qkv_ref, out_ref,
-    columns_ref, grid_s, bias_s, val_s, after_s, own_sem, send_sem, recv_sem,
+    columns_ref, grid_s, bias_s, after_s, own_sem, send_sem, recv_sem,
 ):
     rows, length, width = own_ref.shape
     slabs, cols = after_s.shape[1:3]
@@ -83,7 +85,8 @@
     barrier = pltpu.get_barrier_semaphore()
 
     def greet(k, carry):
-        device = (lax.rem(slab + k, slabs), tile)
+        to = slab + k
+        device = (jnp.where(to >= slabs, to - slabs, to), tile)
         pl.semaphore_signal(barrier, inc=1, device_id=device, device_id_type=MESH)
         return carry
 
@@ -111,14 +114,13 @@
     def _():
         grid_s[:, REACH + length :] = nothing
 
-    val_s[:, width:] = jnp.ones((val_s.shape[0], width), jnp.bfloat16)
     blocks = length // REACH
     occ_row = slab * rows // BLOCK
     first = tile * (length // BLOCK)
     occ = [occupied_at(occ_ref, occ_row, first - 2 + b) for b in range(2 * blocks + 4)]
     for block in range(blocks):
         bias_s[block] = block_bias(occ[2 * block : 2 * block + 6])
-    taps = [[conv_ref[pl.ds(3 * a + b, 1), :] for b in range(3)] for a in range(3)]
+    taps = [[conv_ref[a, pl.ds(b, 1), :] for b in range(3)] for a in range(3)]
     gain = gain_ref[...]
     count = length + 2 * REACH
 
@@ -130,24 +132,17 @@
         convolved = here + middle + pltpu.roll(left, 1, 0) + pltpu.roll(right, count - 1, 0)
         stream = convolved.astype(jnp.bfloat16).astype(jnp.float32)
         normed = norm(stream, gain)
-        queries = jnp.dot(
-            normed[REACH : REACH + length], qkv_ref[:, :width], preferred_element_type=jnp.float32
-        )
-        queries = (queries * SCALE).astype(jnp.bfloat16)
-        key_value = jnp.dot(normed, qkv_ref[:, width:], preferred_element_type=jnp.float32)
-        key_value = key_value.astype(jnp.bfloat16)
-        keys = key_value[:, :width]
-        val_s[:, :width] = key_value[:, width:]
+        queries, keys, values_t = project(normed, qkv_ref, width)
         for block in range(blocks):
             low = block * REACH
-            mixture = attend_block(
-                queries[low : low + REACH],
+            update = attend_block(
+                queries[REACH + low : 2 * REACH + low],
                 keys[low : low + KEYS],
-                val_s[low : low + KEYS],
+                values_t[:, low : low + KEYS],
                 bias_s[block],
                 occ[2 + 2 * block : 4 + 2 * block],
+                out_ref[...],
             )
-            update = jnp.dot(mixture, out_ref[...], preferred_element_type=jnp.float32)
             result = stream[REACH + low : 2 * REACH + low] + update
             after_s[row, low // cols : (low + REACH) // cols] = result.reshape(
                 REACH // cols, cols, width
@@ -165,16 +160,21 @@
             after_s.at[taken, slab], columns_ref.at[place], own_sem.at[group]
         ).start()
 
-        def send(k, carry):
-            step = (k + 1) // 2
-            to = lax.rem(slab + lax.rem(k, 2) * step + (1 - lax.rem(k, 2)) * (slabs - step), slabs)
+        def send(to):
             pltpu.make_async_remote_copy(
                 src_ref=after_s.at[taken, to], dst_ref=columns_ref.at[place],
                 send_sem=send_sem, recv_sem=recv_sem, device_id=(to, tile), device_id_type=MESH,
             ).start()
+
+        def send_both(step, carry):
+            ahead, behind = slab + step, slab - step
+            send(jnp.where(ahead >= slabs, ahead - slabs, ahead))
+            send(jnp.where(behind < 0, behind + slabs, behind))
             return carry
 
-        lax.fori_loop(1, slabs, send, 0)
+        lax.fori_loop(1, slabs // 2, send_both, 0, unroll=3)
+        half = slab + slabs // 2
+        send(jnp.where(half >= slabs, half - slabs, half))
     for group in range(rows // GROUP):
         start = group * GROUP
         pltpu.make_async_copy(
@@ -202,31 +202,26 @@
     gain = gain_ref[...]
     for col in range(cols):
         normed = norm(line_s[pl.ds(col, height, stride=cols), :], gain)
-        queries = jnp.dot(normed, qkv_ref[:, :width], preferred_element_type=jnp.float32)
-        query_s[col] = (queries * SCALE).astype(jnp.bfloat16)
-        key_value = jnp.dot(normed, qkv_ref[:, width:], preferred_element_type=jnp.float32)
-        key_value = key_value.astype(jnp.bfloat16)
-        key_s[col, :REACH] = jnp.zeros((REACH, width), jnp.bfloat16)
-        key_s[col, REACH + height :] = jnp.zeros((REACH, width), jnp.bfloat16)
-        key_s[col, REACH : REACH + height] = key_value[:, :width]
-        val_s[col, :REACH, :width] = jnp.zeros((REACH, width), jnp.bfloat16)
-        val_s[col, REACH + height :, :width] = jnp.zeros((REACH, width), jnp.bfloat16)
-        val_s[col, REACH : REACH + height, :width] = key_value[:, width:]
-        val_s[col, :, width:] = jnp.ones((height + 2 * REACH, width), jnp.bfloat16)
+        query_s[col], keys, values_t = project(normed, qkv_ref, width)
+        edge = jnp.zeros((REACH, width), jnp.bfloat16)
+        key_s[col, :REACH], key_s[col, REACH + height :] = edge, edge
+        val_s[col, :, :REACH], val_s[col, :, REACH + height :] = edge, edge
+        key_s[col, REACH : REACH + height] = keys
+        val_s[col, :, REACH : REACH + height] = values_t
 
     def one_block(block, carry):
         occ = [occupied_at(occ_ref, 2 * block - 2 + b, occ_col) for b in range(6)]
         bias = block_bias(occ)
         low = pl.multiple_of(block * REACH, REACH)
         for col in range(cols):
-            mixture = attend_block(
+            update = attend_block(
                 query_s[col, pl.ds(low, REACH)],
                 key_s[col, pl.ds(low, KEYS)],
-                val_s[col, pl.ds(low, KEYS)],
+                val_s[col, :, pl.ds(low, KEYS)],
                 bias,
                 occ[2:4],
+                out_ref[...],
             )
-            update = jnp.dot(mixture, out_ref[...], preferred_element_type=jnp.float32)
             place = pl.ds(block * (REACH * cols) + col, REACH, stride=cols)
             line_s[place, :] = line_s[place, :] + update
         return carry
@@ -303,8 +298,7 @@
         out_specs=ANY,
         scratch_shapes=[
             pltpu.VMEM((rows + 2, count, width), jnp.float32),
-            pltpu.VMEM((length // REACH, REACH, KEYS), jnp.float32),
-            pltpu.VMEM((count, 2 * width), jnp.bfloat16),
+            pltpu.VMEM((length // REACH, KEYS, REACH), jnp.float32),
             pltpu.VMEM((rows, slabs, cols, width), jnp.bfloat16),
             pltpu.SemaphoreType.DMA((rows // GROUP,)),
             pltpu.SemaphoreType.DMA,
@@ -314,7 +308,7 @@
         name="row_sublayer",
     )(
         occupancy, tokens, top, bottom, left, right,
-        conv_weight.reshape(9, width), row_gain.reshape(1, width), row_qkv, row_out,
+        conv_weight, row_gain.reshape(1, width), row_qkv, row_out,
     )
     mixed = pl.pallas_call(
         col_kernel,
@@ -325,7 +319,7 @@
             pltpu.VMEM((height * cols, width), jnp.float32),
             pltpu.VMEM((cols, height, width), jnp.bfloat16),
             pltpu.VMEM((cols, height + 2 * REACH, width), jnp.bfloat16),
-            pltpu.VMEM((cols, height + 2 * REACH, 2 * width), jnp.bfloat16),
+            pltpu.VMEM((cols, width, height + 2 * REACH), jnp.bfloat16),
         ],
         name="col_sublayer",
     )(occupancy, columns.reshape(height * cols, width), col_gain.reshape(1, width), col_qkv, col_out)

time: 81 us -> 76.3 us (0.942)
  Pallas kernels: 79.5 us -> 76.1 us
  local copies, waits for them, and re-layouts: 1.3 us -> 0 us
    pallas_call x1, Pallas kernels: 15.2 us -> 12.9 us  [local(): pl.pallas_call(col_kernel, out_shape=jax.ShapeDtypeStruct((height * cols,...]
    reshape x1 -> x0, local copies, waits for them, and re-layouts: 1.3 us -> none  [local(): conv_weight.reshape(9, width)]
    pallas_call x1, Pallas kernels: 43.1 us -> 42.1 us  [local(): pl.pallas_call(row_kernel, out_shape=jax.ShapeDtypeStruct((height, cols,...]
where the time goes in v4:
time: 76.3 us; the launch traced here: 76.1 us
  Pallas kernels  76.1 us (100%)
    pallas_call x1, Pallas kernels, local(): pl.pallas_call(row_kernel, out_shape=jax.ShapeDtypeStruct((height, cols,...  42.1 us
    pallas_call x1, Pallas kernels, local(): pl.pallas_call(halo_kernel, out_shape=(edge, edge, side, side), in_specs=...  21.1 us
    pallas_call x1, Pallas kernels, local(): pl.pallas_call(col_kernel, out_shape=jax.ShapeDtypeStruct((height * cols,...  12.9 us

profile of v4, /device:TPU:1, one launch (start us, length us, event | category | flops | bytes accessed | tf_op | source)
XLA Modules:
  0.0 76.1 jit_solution(3161942924693923517)
XLA Ops:
  0.0 21.1 %halo.1 = (bf16[1,256,128]{2,1,0:T(8,128)(2,1)}, bf16[1,256,128]{2,1,0:T(8,128)(2,1)}, bf16[10,128,128]{2,1,0:T(8,128)(2,1)}, bf16[10,128,128]{2,1,0:T(8,128)(2,1)}) custom-call(bf16[8,256,128]{2,1,0:T(8,128)(2,1)} %own_ref.3), custom_call_target="tpu_custom_call" | custom-call | tf_op jit(solution)/shard_map/halo/pallas_call | solution.py:285
  21.1 42.1 %row_sublayer.1 = bf16[1024,2,128]{2,1,0:T(2,128)(2,1)} custom-call(s32[16,16]{1,0:T(8,128)} %occ_ref.3, bf16[8,256,128]{2,1,0:T(8,128)(2,1)} %own_ref.3, bf16[1,256,128]{2,1,0:T(8,128)(2,1)} %get-tuple-element.9.top_ref, bf16[1,256,128]{2,1,0:T(8,128)(2,1)} %get-tuple-element.10.bottom_ref, bf16[10,128,128]{2,1,0:T(8,128)(2,1)} %get-tuple-element.11.left_ref, ...), custom_call_target="tpu_custom_call" | custom-call | tf_op jit(solution)/shard_map/row_sublayer/pallas_call | solution.py:294
  63.2 12.9 %col_sublayer.1 = bf16[2048,128]{1,0:T(8,128)(2,1)} custom-call(s32[16,16]{1,0:T(8,128)} %occ_ref.3, bf16[2048,128]{1,0:T(8,128)(2,1)} %bitcast.4, f32[1,128]{1,0:T(1,128)} %bitcast.6, bf16[128,384]{1,0:T(8,128)(2,1)} %qkv_ref.3, bf16[128,128]{1,0:T(8,128)(2,1)} %out_ref.3), custom_call_target="tpu_custom_call" | custom-call | tf_op jit(solution)/shard_map/col_sublayer/pallas_call | solution.py:313

commit v5 on v4

--- a/solution.py
+++ b/solution.py
@@ -56,6 +56,32 @@
         )
         mixtures.append(mixture * (occupied / total))
     mixture = jnp.concatenate(mixtures, axis=0).T.astype(jnp.bfloat16)
+    return jnp.dot(mixture, out_weight, preferred_element_type=jnp.float32)
+
+
+SPAN = BLOCK + 2 * REACH
+
+
+def attend_small(queries, keys, values_t, bias, out_weight):
+    head = lax.broadcasted_iota(jnp.int32, (BLOCK, 128), 1) // HEAD_DIM
+    zero = jnp.zeros_like(queries)
+    stacked = jnp.concatenate([jnp.where(head == h, queries, zero) for h in range(HEADS)], axis=0)
+    scores = lax.dot_general(
+        keys, stacked, (((1,), (1,)), ((), ())), preferred_element_type=jnp.float32
+    )
+    mixtures = []
+    for pair in range(HEADS // 2):
+        part = scores[:, pair * 128 : (pair + 1) * 128] + bias
+        weights = jnp.exp2(part - jnp.max(part, axis=0, keepdims=True))
+        total = jnp.sum(weights, axis=0, keepdims=True)
+        mixture = jnp.dot(
+            values_t[pair * BLOCK : (pair + 1) * BLOCK],
+            weights.astype(jnp.bfloat16),
+            preferred_element_type=jnp.float32,
+        )
+        mixtures.append(mixture * (1.0 / total))
+    both = jnp.concatenate(mixtures, axis=0).T
+    mixture = jnp.where(head % 2 == 0, both[:BLOCK], both[BLOCK:]).astype(jnp.bfloat16)
     return jnp.dot(mixture, out_weight, preferred_element_type=jnp.float32)
 
 
@@ -191,7 +217,7 @@
     whole.wait_recv()
 
 
-def col_kernel(occ_ref, x_ref, gain_ref, qkv_ref, out_ref, mixed_ref, line_s, query_s, key_s, val_s):
+def col_kernel(occ_ref, x_ref, gain_ref, qkv_ref, out_ref, mixed_ref, line_s, query_s, key_s, val_s, blocks_s):
     count, width = x_ref.shape
     cols = key_s.shape[0]
     height = count // cols
@@ -205,28 +231,65 @@
         query_s[col], keys, values_t = project(normed, qkv_ref, width)
         edge = jnp.zeros((REACH, width), jnp.bfloat16)
         key_s[col, :REACH], key_s[col, REACH + height :] = edge, edge
-        val_s[col, :, :REACH], val_s[col, :, REACH + height :] = edge, edge
         key_s[col, REACH : REACH + height] = keys
-        val_s[col, :, REACH : REACH + height] = values_t
-
-    def one_block(block, carry):
-        occ = [occupied_at(occ_ref, 2 * block - 2 + b, occ_col) for b in range(6)]
-        bias = block_bias(occ)
-        low = pl.multiple_of(block * REACH, REACH)
-        for col in range(cols):
-            update = attend_block(
-                query_s[col, pl.ds(low, REACH)],
-                key_s[col, pl.ds(low, KEYS)],
-                val_s[col, :, pl.ds(low, KEYS)],
+        wide = jnp.concatenate([edge, values_t, edge], axis=1)
+        val_s[0, col] = wide
+        val_s[1, col, :, : height + REACH] = wide[:, BLOCK : BLOCK + height + REACH]
+        val_s[1, col, :, height + REACH :] = edge
+
+    at = lax.broadcasted_iota(jnp.int32, (SPAN, 128), 0)
+    offset = lax.broadcasted_iota(jnp.int32, (SPAN, 128), 1) % BLOCK - (at - REACH)
+    band = jnp.where(jnp.abs(offset) < REACH, jnp.float32(0.0), jnp.float32(NEG))
+
+    total_blocks = height // BLOCK
+
+    def note(block, found):
+        blocks_s[found] = block
+        return found + jnp.where(occupied_at(occ_ref, block, occ_col) > 0, 1, 0)
+
+    found = lax.fori_loop(0, total_blocks, note, 0)
+
+    @pl.when(found < total_blocks)
+    def _():
+        blocks_s[found] = 0
+
+    def updates_of(block):
+        occ = [occupied_at(occ_ref, block - 2 + b, occ_col) for b in range(5)]
+        barred = [
+            jnp.full((BLOCK, 128), jnp.where(value > 0, jnp.float32(0.0), jnp.float32(NEG)))
+            for value in occ
+        ]
+        bias = jnp.where(offset == 0, 0.0, jnp.minimum(band, jnp.concatenate(barred, axis=0)))
+        low = pl.multiple_of(block * BLOCK, BLOCK)
+        wide_low = pl.multiple_of(block // 2 * REACH, REACH)
+        return [
+            attend_small(
+                query_s[col, pl.ds(low, BLOCK)],
+                key_s[col, pl.ds(low, SPAN)],
+                val_s[block % 2, col, :, pl.ds(wide_low, KEYS)][:, :SPAN],
                 bias,
-                occ[2:4],
                 out_ref[...],
             )
-            place = pl.ds(block * (REACH * cols) + col, REACH, stride=cols)
-            line_s[place, :] = line_s[place, :] + update
+            for col in range(cols)
+        ]
+
+    def add(block, updates):
+        for col in range(cols):
+            place = pl.ds(block * (BLOCK * cols) + col, BLOCK, stride=cols)
+            line_s[place, :] = line_s[place, :] + updates[col]
+
+    def two_blocks(pair, carry):
+        one, two = blocks_s[2 * pair], blocks_s[2 * pair + 1]
+        first, second = updates_of(one), updates_of(two)
+        add(one, first)
+
+        @pl.when(2 * pair + 1 < found)
+        def _():
+            add(two, second)
+
         return carry
 
-    lax.fori_loop(0, height // REACH, one_block, 0)
+    lax.fori_loop(0, (found + 1) // 2, two_blocks, 0)
     mixed_ref[...] = line_s[...].astype(jnp.bfloat16)
 
 
@@ -319,7 +382,8 @@
             pltpu.VMEM((height * cols, width), jnp.float32),
             pltpu.VMEM((cols, height, width), jnp.bfloat16),
             pltpu.VMEM((cols, height + 2 * REACH, width), jnp.bfloat16),
-            pltpu.VMEM((cols, width, height + 2 * REACH), jnp.bfloat16),
+            pltpu.VMEM((2, cols, width, height + 2 * REACH), jnp.bfloat16),
+            pltpu.SMEM((height // BLOCK,), jnp.int32),
         ],
         name="col_sublayer",
     )(occupancy, columns.reshape(height * cols, width), col_gain.reshape(1, width), col_qkv, col_out)

time: 76.3 us -> 73.7 us (0.966); the launches traced: 76.1 us -> 72.5 us
  Pallas kernels: 76.1 us -> 72.5 us
    pallas_call x1, Pallas kernels: 12.9 us -> 9.25 us  [local(): pl.pallas_call(col_kernel, out_shape=jax.ShapeDtypeStruct((height * cols,...]
where the time goes in v5:
time: 73.7 us; the launch traced here: 72.5 us
  Pallas kernels  72.5 us (98%)
    pallas_call x1, Pallas kernels, local(): pl.pallas_call(row_kernel, out_shape=jax.ShapeDtypeStruct((height, cols,...  42.1 us
    pallas_call x1, Pallas kernels, local(): pl.pallas_call(halo_kernel, out_shape=(edge, edge, side, side), in_specs=...  21.1 us
    pallas_call x1, Pallas kernels, local(): pl.pallas_call(col_kernel, out_shape=jax.ShapeDtypeStruct((height * cols,...  9.25 us

profile of v5, /device:TPU:1, one launch (start us, length us, event | category | flops | bytes accessed | tf_op | source)
XLA Modules:
  0.0 72.5 jit_solution(17385537364214085006)
XLA Ops:
  0.0 21.1 %halo.1 = (bf16[1,256,128]{2,1,0:T(8,128)(2,1)}, bf16[1,256,128]{2,1,0:T(8,128)(2,1)}, bf16[10,128,128]{2,1,0:T(8,128)(2,1)}, bf16[10,128,128]{2,1,0:T(8,128)(2,1)}) custom-call(bf16[8,256,128]{2,1,0:T(8,128)(2,1)} %own_ref.3), custom_call_target="tpu_custom_call" | custom-call | tf_op jit(solution)/shard_map/halo/pallas_call | solution.py:348
  21.1 42.1 %row_sublayer.1 = bf16[1024,2,128]{2,1,0:T(2,128)(2,1)} custom-call(s32[16,16]{1,0:T(8,128)} %occ_ref.3, bf16[8,256,128]{2,1,0:T(8,128)(2,1)} %own_ref.3, bf16[1,256,128]{2,1,0:T(8,128)(2,1)} %get-tuple-element.9.top_ref, bf16[1,256,128]{2,1,0:T(8,128)(2,1)} %get-tuple-element.10.bottom_ref, bf16[10,128,128]{2,1,0:T(8,128)(2,1)} %get-tuple-element.11.left_ref, ...), custom_call_target="tpu_custom_call" | custom-call | tf_op jit(solution)/shard_map/row_sublayer/pallas_call | solution.py:357
  63.2 9.3 %col_sublayer.1 = bf16[2048,128]{1,0:T(8,128)(2,1)} custom-call(s32[16,16]{1,0:T(8,128)} %occ_ref.3, bf16[2048,128]{1,0:T(8,128)(2,1)} %bitcast.4, f32[1,128]{1,0:T(1,128)} %bitcast.6, bf16[128,384]{1,0:T(8,128)(2,1)} %qkv_ref.3, bf16[128,128]{1,0:T(8,128)(2,1)} %out_ref.3), custom_call_target="tpu_custom_call" | custom-call | tf_op jit(solution)/shard_map/col_sublayer/pallas_call | solution.py:376

commit v6 on v5

--- a/solution.py
+++ b/solution.py
@@ -12,7 +12,7 @@
 BLOCK = 64
 REACH = 128
 KEYS = 3 * REACH
-GROUP = 4
+GROUP = 2
 NEG = -1e30
 SCALE = math.log2(math.e) / math.sqrt(HEAD_DIM)
 

time: 73.7 us -> 69.9 us (0.948)
  the two profiles are of different devices: /device:TPU:1 before, /device:TPU:17 now
where the time goes in v6:
time: 69.9 us; the launch traced here: 69.8 us
  Pallas kernels  69.8 us (100%)
    pallas_call x1, Pallas kernels, local(): pl.pallas_call(row_kernel, out_shape=jax.ShapeDtypeStruct((height, cols,...  41 us
    pallas_call x1, Pallas kernels, local(): pl.pallas_call(halo_kernel, out_shape=(edge, edge, side, side), in_specs=...  18.1 us
    pallas_call x1, Pallas kernels, local(): pl.pallas_call(col_kernel, out_shape=jax.ShapeDtypeStruct((height * cols,...  10.7 us

profile of v6, /device:TPU:17, one launch (start us, length us, event | category | flops | bytes accessed | tf_op | source)
XLA Modules:
  0.0 69.8 jit_solution(5406338825361974426)
XLA Ops:
  0.0 18.1 %halo.1 = (bf16[1,256,128]{2,1,0:T(8,128)(2,1)}, bf16[1,256,128]{2,1,0:T(8,128)(2,1)}, bf16[10,128,128]{2,1,0:T(8,128)(2,1)}, bf16[10,128,128]{2,1,0:T(8,128)(2,1)}) custom-call(bf16[8,256,128]{2,1,0:T(8,128)(2,1)} %own_ref.3), custom_call_target="tpu_custom_call" | custom-call | tf_op jit(solution)/shard_map/halo/pallas_call | solution.py:348
  18.1 41.0 %row_sublayer.1 = bf16[1024,2,128]{2,1,0:T(2,128)(2,1)} custom-call(s32[16,16]{1,0:T(8,128)} %occ_ref.3, bf16[8,256,128]{2,1,0:T(8,128)(2,1)} %own_ref.3, bf16[1,256,128]{2,1,0:T(8,128)(2,1)} %get-tuple-element.9.top_ref, bf16[1,256,128]{2,1,0:T(8,128)(2,1)} %get-tuple-element.10.bottom_ref, bf16[10,128,128]{2,1,0:T(8,128)(2,1)} %get-tuple-element.11.left_ref, ...), custom_call_target="tpu_custom_call" | custom-call | tf_op jit(solution)/shard_map/row_sublayer/pallas_call | solution.py:357
  59.1 10.7 %col_sublayer.1 = bf16[2048,128]{1,0:T(8,128)(2,1)} custom-call(s32[16,16]{1,0:T(8,128)} %occ_ref.3, bf16[2048,128]{1,0:T(8,128)(2,1)} %bitcast.4, f32[1,128]{1,0:T(1,128)} %bitcast.6, bf16[128,384]{1,0:T(8,128)(2,1)} %qkv_ref.3, bf16[128,128]{1,0:T(8,128)(2,1)} %out_ref.3), custom_call_target="tpu_custom_call" | custom-call | tf_op jit(solution)/shard_map/col_sublayer/pallas_call | solution.py:376

commit v7 on v6

--- a/solution.py
+++ b/solution.py
@@ -193,14 +193,15 @@
             ).start()
 
         def send_both(step, carry):
-            ahead, behind = slab + step, slab - step
+            away = slabs // 2 - step
+            ahead, behind = slab + away, slab - away
             send(jnp.where(ahead >= slabs, ahead - slabs, ahead))
             send(jnp.where(behind < 0, behind + slabs, behind))
             return carry
 
-        lax.fori_loop(1, slabs // 2, send_both, 0, unroll=3)
         half = slab + slabs // 2
         send(jnp.where(half >= slabs, half - slabs, half))
+        lax.fori_loop(1, slabs // 2, send_both, 0, unroll=3)
     for group in range(rows // GROUP):
         start = group * GROUP
         pltpu.make_async_copy(

time: 69.9 us -> 70.6 us (1.010)
  the two profiles are of different devices: /device:TPU:17 before, /device:TPU:7 now
where the time goes in v7:
time: 70.6 us; the launch traced here: 69.6 us
  Pallas kernels  69.6 us (99%)
    pallas_call x1, Pallas kernels, local(): pl.pallas_call(row_kernel, out_shape=jax.ShapeDtypeStruct((height, cols,...  39 us
    pallas_call x1, Pallas kernels, local(): pl.pallas_call(halo_kernel, out_shape=(edge, edge, side, side), in_specs=...  19.9 us
    pallas_call x1, Pallas kernels, local(): pl.pallas_call(col_kernel, out_shape=jax.ShapeDtypeStruct((height * cols,...  10.7 us

profile of v7, /device:TPU:7, one launch (start us, length us, event | category | flops | bytes accessed | tf_op | source)
XLA Modules:
  0.0 69.6 jit_solution(2125869602774821930)
XLA Ops:
  0.0 19.9 %halo.1 = (bf16[1,256,128]{2,1,0:T(8,128)(2,1)}, bf16[1,256,128]{2,1,0:T(8,128)(2,1)}, bf16[10,128,128]{2,1,0:T(8,128)(2,1)}, bf16[10,128,128]{2,1,0:T(8,128)(2,1)}) custom-call(bf16[8,256,128]{2,1,0:T(8,128)(2,1)} %own_ref.3), custom_call_target="tpu_custom_call" | custom-call | tf_op jit(solution)/shard_map/halo/pallas_call | solution.py:349
  19.9 39.0 %row_sublayer.1 = bf16[1024,2,128]{2,1,0:T(2,128)(2,1)} custom-call(s32[16,16]{1,0:T(8,128)} %occ_ref.3, bf16[8,256,128]{2,1,0:T(8,128)(2,1)} %own_ref.3, bf16[1,256,128]{2,1,0:T(8,128)(2,1)} %get-tuple-element.9.top_ref, bf16[1,256,128]{2,1,0:T(8,128)(2,1)} %get-tuple-element.10.bottom_ref, bf16[10,128,128]{2,1,0:T(8,128)(2,1)} %get-tuple-element.11.left_ref, ...), custom_call_target="tpu_custom_call" | custom-call | tf_op jit(solution)/shard_map/row_sublayer/pallas_call | solution.py:358
  59.0 10.7 %col_sublayer.1 = bf16[2048,128]{1,0:T(8,128)(2,1)} custom-call(s32[16,16]{1,0:T(8,128)} %occ_ref.3, bf16[2048,128]{1,0:T(8,128)(2,1)} %bitcast.4, f32[1,128]{1,0:T(1,128)} %bitcast.6, bf16[128,384]{1,0:T(8,128)(2,1)} %qkv_ref.3, bf16[128,128]{1,0:T(8,128)(2,1)} %out_ref.3), custom_call_target="tpu_custom_call" | custom-call | tf_op jit(solution)/shard_map/col_sublayer/pallas_call | solution.py:377
